TPU v7x, 32 devices: a whole 2x2x4 slice. The times are simulated.
32 devices in a mesh: grp: 2 (over x), wave: 16 (over z, y, core).
Axes of the slice: x: 2, y: 2, z: 4, core: 2. Of those that a mesh axis runs over, the one named last changes fastest.
Arguments:
- spectral: bfloat16 [640, 641, 256], P(('grp', 'wave')), parts along dimension 0, may hold values from -0.23925781 to 0.23925781
- legendre: bfloat16 [320, 641, 320], P('wave'), may hold values from -0.25 to 0.25
- pair_low: int32 [320], replicated, may hold values from 0 to 319, each once
- routes: int32 [102400, 1], P(('grp', 'wave')), parts along dimension 0, may hold values from 0 to 15; in each aligned block of 3200 rows (0 to 3199, 3200 to 6399, ...) at most 400 rows name the same one
- w_in: bfloat16 [16, 128, 1024], P('wave'), may hold values from -0.5 to 0.5
- w_mid: bfloat16 [16, 1024, 1024], P('wave'), may hold values from -0.1875 to 0.1875
- w_out: bfloat16 [16, 1024, 128], P('wave'), may hold values from -1.5 to 1.5
Outputs:
- tendency: bfloat16 [640, 641, 256], P(('grp', 'wave')), parts along dimension 0
There are 2 independent parts, one for each index of `grp`. A program takes and returns all parts, laid end to end along the dimension named above; an argument that names none is the same for every part. Nothing has to cross between parts.
Inputs may be any that keep to these rules, and one draw needn't show every extreme that they name: `routes`: among the columns of one device (each aligned block of 3200 columns) at most 400 name the same network, a bound that some block reaches of them.
All inputs are finite; a program needn't handle non-finite values.
Results may differ from a plain program's by a relative error of at most 0.01.
Values may be sent and summed in bfloat16 or wider, within the bound.
A program may use at most 192 MiB of HBM per device.

v0:
```python
import math

import jax
import jax.numpy as jnp
from jax import lax
from jax.sharding import PartitionSpec as P

NLON = 1280
FIELDS = 4


def slot_waves(pair_low, wave_total):
    return jnp.stack([pair_low, wave_total - 1 - pair_low], axis=1).reshape(-1)


def side_masks(pair_low, wave_total):
    degree = jnp.arange(wave_total + 1, dtype=jnp.int32)
    lower_side = degree[None, :] < (wave_total - pair_low)[:, None]
    return jnp.stack([lower_side, jnp.logical_not(lower_side)], axis=1)


def fourier_table(wavenums, points, inverse):
    longitude = jnp.arange(points, dtype=jnp.int32)
    phases = wavenums[:, None] * longitude[None, :] % points
    angles = phases.astype(jnp.float32) * jnp.float32(2.0 * math.pi / points)
    if inverse:
        factor = jnp.where(wavenums == 0, jnp.float32(1.0), jnp.float32(2.0))[:, None]
    else:
        factor = jnp.full((wavenums.shape[0], 1), 1.0 / math.sqrt(points), jnp.float32)
    return jnp.stack([factor * jnp.cos(angles), -factor * jnp.sin(angles)], axis=1).astype(
        jnp.bfloat16
    )


def forcing(grid_fields):
    flattened = grid_fields.reshape(FIELDS, -1)
    return (flattened * jnp.roll(flattened, -1, axis=0)).reshape(grid_fields.shape)


def coarse_columns(grid_fields):
    feat_width = grid_fields.shape[0]
    lat_rows = grid_fields.shape[1]
    lon_count = grid_fields.shape[2]
    blocks = grid_fields.reshape(feat_width, lat_rows // 2, 2, lon_count // 4, 4).mean(axis=(2, 4))
    return blocks.reshape(feat_width, -1).T.astype(jnp.bfloat16)


def spread_back(values, lat_rows):
    feat_width = values.shape[1]
    coarse = values.astype(jnp.float32).T.reshape(feat_width, lat_rows // 2, -1)
    before = jnp.roll(coarse, 1, axis=2)
    following = jnp.roll(coarse, -1, axis=2)
    pieces = [
        0.375 * before + 0.625 * coarse,
        0.125 * before + 0.875 * coarse,
        0.875 * coarse + 0.125 * following,
        0.625 * coarse + 0.375 * following,
    ]
    fine_grid = jnp.stack(pieces, axis=3).reshape(feat_width, lat_rows // 2, -1)
    return jnp.repeat(fine_grid, 2, axis=1)


def slot_positions(regimes, experts_total):
    onehot = (regimes[:, :, None] == jnp.arange(experts_total, dtype=jnp.int32)).astype(jnp.int32)
    ranking = jnp.cumsum(onehot, axis=1) - 1
    return jnp.sum(ranking * onehot, axis=2)


def network(columns, weight_in, weight_mid, weight_out):
    hidden = jax.nn.silu(jnp.dot(columns, weight_in, preferred_element_type=jnp.float32)).astype(
        jnp.bfloat16
    )
    deeper = jax.nn.silu(jnp.dot(hidden, weight_mid, preferred_element_type=jnp.float32)).astype(
        jnp.bfloat16
    )
    return jnp.dot(deeper, weight_out, preferred_element_type=jnp.float32).astype(jnp.bfloat16)


def masked_inverse(spectral, legendre, side_mask):
    masked = jnp.where(side_mask[:, :, :, None], spectral[:, None], jnp.zeros((), jnp.bfloat16))
    return jnp.einsum("psjc,pjl->pscl", masked, legendre, preferred_element_type=jnp.float32)


def masked_forward(legendre, coeffs, side_mask):
    both_sides = jnp.einsum(
        "pjl,pskrl->psjkr", legendre, coeffs, preferred_element_type=jnp.float32
    )
    return jnp.sum(jnp.where(side_mask[:, :, :, None, None], both_sides, 0.0), axis=1)


def on_device(spectral, legendre, pair_low, routes, w_in, w_mid, w_out):
    pair_count = spectral.shape[0]
    degrees = spectral.shape[1]
    channels = spectral.shape[2]
    feat_width = channels // 2
    lat_total = legendre.shape[2]
    wave_total = degrees - 1
    devices = lax.axis_size("wave")
    local_low = lax.dynamic_slice_in_dim(pair_low, lax.axis_index("wave") * pair_count, pair_count)
    side_mask = side_masks(local_low, wave_total)
    inverse_out = masked_inverse(spectral, legendre, side_mask)
    fourier_in = inverse_out.astype(jnp.bfloat16).reshape(2 * pair_count, feat_width, 2, lat_total)
    wavenums = slot_waves(pair_low, wave_total)
    inverse_table = fourier_table(wavenums, NLON, True)
    grid_fields = jnp.einsum(
        "qkra,qrl->kal",
        lax.all_to_all(fourier_in, "wave", split_axis=3, concat_axis=0, tiled=True),
        inverse_table,
        preferred_element_type=jnp.float32,
    )
    lat_rows = grid_fields.shape[1]
    forced = forcing(grid_fields)
    columns = coarse_columns(grid_fields)
    regimes = routes[:, 0].reshape(1, -1)
    positions = slot_positions(regimes, devices)[0]
    regime_row = regimes[0]
    capacity = 2 * columns.shape[0] // devices
    outgoing = (
        jnp.zeros((devices, capacity, feat_width), jnp.bfloat16)
        .at[regime_row, positions]
        .set(columns)
    )
    arrived = lax.all_to_all(outgoing, "wave", split_axis=0, concat_axis=0, tiled=True)
    answers = network(arrived.reshape(-1, feat_width), w_in[0], w_mid[0], w_out[0]).reshape(
        arrived.shape
    )
    incoming = lax.all_to_all(answers, "wave", split_axis=0, concat_axis=0, tiled=True)
    returned = incoming[regime_row, positions]
    correction = spread_back(returned, lat_rows)
    tendency_grid = (forced + correction).astype(jnp.bfloat16)
    forward_table = fourier_table(wavenums, NLON, False)
    fourier_out = jnp.einsum(
        "fal,qrl->qfra", tendency_grid, forward_table, preferred_element_type=jnp.float32
    ).astype(jnp.bfloat16)
    received = lax.all_to_all(fourier_out, "wave", split_axis=0, concat_axis=3, tiled=True)
    coeffs = received.reshape(pair_count, 2, received.shape[1], 2, received.shape[3])
    result = masked_forward(legendre, coeffs, side_mask)
    spectral_out = result.astype(jnp.bfloat16)
    return spectral_out.reshape(pair_count, degrees, channels)


def solution(mesh):
    placed = (
        P(("grp", "wave"), None, None),
        P("wave", None, None),
        P(),
        P(("grp", "wave"), None),
        P("wave", None, None),
        P("wave", None, None),
        P("wave", None, None),
    )
    return jax.shard_map(
        on_device,
        mesh=mesh,
        in_specs=placed,
        out_specs=P(("grp", "wave"), None, None),
        check_vma=False,
    )
```

profile of v0, /device:TPU:1, one launch (start us, length us, event | category | flops | bytes accessed | tf_op | source)
XLA Modules:
  0.0 719.1 jit_solution(5438922527559547650)
XLA Ops:
  0.0 0.9 dynamic-slice_subtract_fusion
  0.9 0.2 iota_compare_fusion.1
  1.1 0.2 pad_add_fusion
  1.3 0.6 copy-done.7
  1.9 10.8 %fusion.11 = bf16[20,2,256,320]{2,3,1,0:T(8,128)(2,1)} fusion(bf16[20,641,320]{1,2,0:T(8,128)(2,1)} %param.8, pred[20,2,641]{2,1,0:T(4,128)(4,1)S(1)} %pad_add_fusion, bf16[20,641,256]{2,1,0:T(8,128)(2,1)} %param.7), kind=kOutput, calls=%fused_computation.19 | convolution fusion | flops 4210698240 | bytes 21347880 | tf_op jit(solution)/shard_map/psjc,pjl->pscl/dot_general | solution.py:81
  12.7 9.8 %copy.121 = bf16[20,2,256,320]{3,2,1,0:T(8,128)(2,1)} copy(bf16[20,2,256,320]{2,3,1,0:T(8,128)(2,1)} %fusion.11) | data formatting | bytes 13107200 | tf_op jit(solution)/shard_map/convert_element_type | solution.py:102
  22.5 16.4 %reshape.601 = bf16[40,128,2,320]{3,2,1,0:T(2,128)(2,1)} reshape(bf16[20,2,256,320]{3,2,1,0:T(8,128)(2,1)} %copy.121) | data formatting | bytes 13107200 | tf_op jit(solution)/shard_map/reshape | solution.py:102
  38.8 14.4 %copy.122 = bf16[40,128,2,320]{1,0,2,3:T(8,128)(2,1)} copy(bf16[40,128,2,320]{3,2,1,0:T(2,128)(2,1)} %reshape.601) | data formatting | bytes 13107200 | tf_op jit(solution)/shard_map/reshape | solution.py:102
  53.2 7.8 %all-to-all-start = ((bf16[40,128,2,320]{1,0,2,3:T(8,128)(2,1)}), bf16[40,128,2,320]{1,0,2,3:T(8,128)(2,1)}, u32[]{:S(2)}, u32[]{:S(2)}) async-start(bf16[40,128,2,320]{1,0,2,3:T(8,128)(2,1)} %copy.122), calls=%async_computation | async-start | bytes 13107200 | tf_op jit(solution)/shard_map/all_to_all | solution.py:107
  61.0 0.0 copy-done.10
  61.0 0.0 copy-start.12
  61.0 0.0 copy-start.11
  61.1 0.1 copy.120
  61.2 0.1 mul.201
  61.5 4.6 reduce-window.6
  66.2 0.5 slice_reduce_fusion
  66.6 0.2 reduce-window.9
  66.8 0.1 broadcast.422
  67.0 0.1 fusion.44
  67.1 0.7 or_reduce_fusion
  67.8 0.1 multiply_reduce_fusion
  67.9 0.1 and_reduce_fusion
  68.0 16.9 %multiply_convert_fusion.9 = (bf16[640,1,1280]{2,0,1:T(8,128)(2,1)}, bf16[640,1,1280]{2,0,1:T(8,128)(2,1)}, bf16[640,1,1280]{2,0,1:T(8,128)(2,1)}, bf16[640,1,1280]{2,0,1:T(8,128)(2,1)}) fusion(s32[640]{0:T(1024)S(1)} %mul.201, f32[640]{0:T(1024)S(1)} %get-tuple-element.23, f32[640]{0:T(1024)S(1)} %get-tuple-element.22), kind=kLoop, calls=%fused_computation.40 | loop fusion | flops 13926400 | bytes 6561280 | tf_op jit(solution)/shard_map/convert.5
  84.9 95.2 %all-to-all-done = bf16[40,128,2,320]{1,0,2,3:T(8,128)(2,1)} async-done(((bf16[40,128,2,320]{1,0,2,3:T(8,128)(2,1)}), bf16[40,128,2,320]{1,0,2,3:T(8,128)(2,1)}, u32[]{:S(2)}, u32[]{:S(2)}) %all-to-all-start) | async-done | bytes 6553632 | tf_op jit(solution)/shard_map/all_to_all | solution.py:107
  180.1 4.8 copy.124
  185.0 11.8 %convolution_bitcast_fusion = f32[128,20,1280]{2,0,1:T(8,128)} fusion(bf16[640,128,2,20]{1,0,3,2:T(8,128)(2,1)S(1)} %bitcast.126, bf16[640,1,1280]{2,0,1:T(8,128)(2,1)S(1)} %copy-done.5, bf16[640,1,1280]{2,0,1:T(8,128)(2,1)S(1)} %copy-done.6), kind=kOutput, calls=%fused_computation.18 | convolution fusion | flops 8390246400 | bytes 22937600 | tf_op jit(solution)/shard_map/qkra,qrl->kal/dot_general | solution.py:105
  196.7 13.9 %copy.129 = f32[128,20,1280]{0,2,1:T(8,128)} copy(f32[128,20,1280]{2,0,1:T(8,128)} %convolution_bitcast_fusion) | data formatting | bytes 26214400 | tf_op jit(solution)/shard_map/qkra,qrl->kal/dot_general | solution.py:105
  210.6 18.5 %reduce_sum.31 = f32[128,10,320]{0,2,1:T(8,128)} reduce(f32[128,10,2,320,4]{0,4,3,2,1:T(4,128)} %bitcast.116, f32[]{:T(128)} %constant.64.clone.1), dimensions={2,4}, to_apply=%region_3.4 | reduce | flops 2867200 | bytes 14745604 | tf_op jit(solution)/shard_map/reduce_sum | solution.py:44
  229.1 1.6 multiply_convert_fusion.10
  230.7 14.9 %scatter_custom_fusion = bf16[6400,128]{1,0:T(8,128)(2,1)} fusion(s32[3200]{0:T(1024)S(1)} %broadcast_select_fusion, bf16[3200,128]{1,0:T(8,128)(2,1)S(1)} %bitcast.130, bf16[]{:T(256)} %constant.19.clone.1), kind=kCustom, calls=%fused_computation.63 | custom fusion | bytes 1638402
  245.7 28.9 %all-to-all-start.1 = ((bf16[16,400,128]{2,1,0:T(8,128)(2,1)}), bf16[16,400,128]{2,1,0:T(8,128)(2,1)}, u32[]{:S(2)}, u32[]{:S(2)}) async-start(bf16[16,400,128]{2,1,0:T(8,128)(2,1)} %bitcast.128), calls=%async_computation.1 | async-start | bytes 3276800 | tf_op jit(solution)/shard_map/all_to_all | solution.py:123
  274.6 4.7 slice.48
  279.3 3.9 slice.49
  283.2 10.1 %copy.126 = f32[96,20,1280]{2,1,0:T(8,128)} copy(f32[96,20,1280]{2,0,1:T(8,128)S(1)} %slice.48) | data formatting | bytes 19660800 | tf_op jit(solution)/shard_map/jit(_roll_static)/slice | solution.py:37
  293.3 14.8 %slice.37 = f32[3,819200]{1,0:T(4,128)} reshape(f32[96,20,1280]{2,1,0:T(8,128)} %copy.126) | data formatting | bytes 19660800 | tf_op jit(solution)/shard_map/jit(_roll_static)/slice | solution.py:37
  308.1 5.8 copy.127
  313.9 7.2 slice.39
  321.0 0.0 all-to-all-done.1
  321.0 0.0 copy-start.14
  321.1 24.3 %fusion.4 = f32[6400,1024]{1,0:T(8,128)} fusion(bf16[6400,128]{1,0:T(8,128)(2,1)} %bitcast.18, bf16[1,1024,1024]{2,1,0:T(8,128)(2,1)S(1)} %copy-done, bf16[1,128,1024]{2,1,0:T(8,128)(2,1)S(1)} %copy-done.13), kind=kOutput, calls=%fused_computation.12 | convolution fusion | flops 15132262400 | bytes 30212096 | tf_op jit(solution)/shard_map/dot_general | solution.py:73
  345.4 12.9 %fusion.10 = bf16[6400,128]{1,0:T(8,128)(2,1)} fusion(f32[6400,1024]{1,0:T(8,128)} %fusion.4, bf16[1,1024,128]{2,1,0:T(8,128)(2,1)S(1)} %copy-done.14), kind=kOutput, calls=%fused_computation.17 | convolution fusion | flops 1711308800 | bytes 28114944 | tf_op jit(solution)/shard_map/dot_general | solution.py:76
  358.3 6.0 all-to-all-start.2
  364.3 15.7 %pad_maximum_fusion = f32[4,819200]{1,0:T(4,128)} fusion(f32[1,819200]{1,0:T(1,128)} %slice.39, f32[3,819200]{1,0:T(4,128)} %slice.37), kind=kLoop, calls=%fused_computation.8 | loop fusion | flops 3276800 | bytes 26214400 | tf_op jit(solution)/shard_map/jit(_roll_static)/concatenate | solution.py:37
  380.1 26.9 %concatenate.55 = f32[128,20,1280]{2,1,0:T(8,128)} reshape(f32[4,819200]{1,0:T(4,128)} %pad_maximum_fusion) | data formatting | bytes 26214400 | tf_op jit(solution)/shard_map/jit(_roll_static)/concatenate | solution.py:37
  407.0 0.0 all-to-all-done.2
  407.0 17.6 %gather_fusion = bf16[3200,128]{1,0:T(8,128)(2,1)S(1)} fusion(bf16[16,400,128]{2,1,0:T(8,128)(2,1)S(1)} %all-to-all-done.2, s32[3200]{0:T(1024)S(1)} %copy-done.2), kind=kCustom, calls=%fused_computation | custom fusion | bytes 1664000 | tf_op jit(solution)/shard_map/gather | solution.py:128
  424.6 0.1 convert_element_type.97
  424.7 0.2 bitcast_multiply_fusion.3
  424.9 0.3 slice_bitcast_fusion.1
  425.3 0.4 fusion.38
  425.7 0.4 multiply_add_fusion.1
  426.1 0.6 pad_maximum_fusion.1
  426.7 7.0 copy.137
  433.7 8.1 %copy.138 = f32[128,10,1280]{2,0,1:T(8,128)} copy(f32[128,10,1280]{0,2,1:T(8,128)} %bitcast.117) | data formatting | bytes 13107200 | tf_op jit(solution)/shard_map/reshape | solution.py:59
  441.8 14.1 %fusion.3 = bf16[128,20,1280]{2,0,1:T(8,128)(2,1)S(1)} fusion(f32[128,20,1280]{2,0,1:T(8,128)} %convolution_bitcast_fusion, f32[128,20,1280]{2,1,0:T(8,128)} %concatenate.55, f32[128,10,1280]{2,0,1:T(8,128)} %copy.138), kind=kLoop, calls=%fused_computation.10 | loop fusion | flops 9830400 | bytes 39321600 | tf_op jit(solution)/shard_map/convert_element_type | solution.py:130
  456.0 9.2 %convert_bitcast_fusion.1 = bf16[640,128,2,20]{1,0,3,2:T(8,128)(2,1)S(1)} fusion(bf16[128,20,1280]{2,0,1:T(8,128)(2,1)S(1)} %fusion.3, bf16[640,1,1280]{2,0,1:T(8,128)(2,1)S(1)} %copy-done.4, bf16[640,1,1280]{2,0,1:T(8,128)(2,1)S(1)} %copy-done.3), kind=kOutput, calls=%fused_computation.27 | convolution fusion | flops 8398438400 | bytes 16384000 | tf_op jit(solution)/shard_map/fal,qrl->qfra/dot_general | solution.py:132
  465.3 38.3 %copy.139 = bf16[640,128,2,20]{1,2,3,0:T(2,128)(2,1)S(1)} copy(bf16[640,128,2,20]{1,0,3,2:T(8,128)(2,1)S(1)} %convert_bitcast_fusion.1) | data formatting | bytes 13107200 | tf_op jit(solution)/shard_map/convert_element_type | solution.py:134
  503.5 150.0 %all_to_all.43 = bf16[640,128,2,20]{1,2,3,0:T(2,128)(2,1)S(1)} all-to-all(bf16[640,128,2,20]{1,2,3,0:T(2,128)(2,1)S(1)} %copy.139), channel_id=1, replica_groups=mesh['grp'=2,'wave'=16] {'wave'}, dimensions={0} | all-to-all | bytes 13107200 | tf_op jit(solution)/shard_map/all_to_all | solution.py:135
  653.6 1.6 copy.140
  655.2 1.1 copy.141
  656.3 15.6 %select_reduce_fusion = bf16[20,128,2,641]{1,3,2,0:T(8,128)(2,1)} fusion(pred[20,2,641]{2,1,0:T(4,128)(4,1)S(1)} %copy-done.8, bf16[20,641,320]{1,2,0:T(8,128)(2,1)} %param.8, bf16[20,2,128,2,320]{2,1,0,4,3:T(2,128)(2,1)S(1)} %bitcast.127), kind=kOutput, calls=%fused_computation.2 | convolution fusion | flops 4210703360 | bytes 21347880 | tf_op jit(solution)/shard_map/pjl,pskrl->psjkr/dot_general | solution.py:85
  671.9 19.9 %copy.143 = bf16[20,641,128,2]{1,3,2,0:T(2,128)(2,1)} copy(bf16[20,641,128,2]{2,1,3,0:T(8,128)(2,1)} %bitcast.125) | data formatting | bytes 13127680 | tf_op jit(solution)/shard_map/convert_element_type | solution.py:138
  691.8 16.9 %convert_element_type.96 = bf16[20,641,256]{1,2,0:T(8,128)(2,1)} reshape(bf16[20,641,128,2]{1,3,2,0:T(2,128)(2,1)} %copy.143) | data formatting | bytes 13127680 | tf_op jit(solution)/shard_map/convert_element_type | solution.py:138
  708.8 10.1 %copy.144 = bf16[20,641,256]{2,1,0:T(8,128)(2,1)} copy(bf16[20,641,256]{1,2,0:T(8,128)(2,1)} %convert_element_type.96) | data formatting | bytes 13127680 | tf_op jit(solution)/shard_map/convert_element_type | solution.py:138
  (38 shorter events, 0.3 us)
Async XLA Ops:
  0.0 321.0 %copy-start = (bf16[1,1024,1024]{2,1,0:T(8,128)(2,1)S(1)}, bf16[1,1024,1024]{2,1,0:T(8,128)(2,1)}, u32[]{:S(2)}) copy-start(bf16[1,1024,1024]{2,1,0:T(8,128)(2,1)} %param.12) | copy-start | bytes 6291460
  1.3 0.6 copy-start.7
  53.2 7.8 %copy-start.10 = (s32[320]{0:T(512)S(1)}, s32[320]{0:T(512)}, u32[]{:S(2)}) copy-start(s32[320]{0:T(512)} %param.9) | copy-start | bytes 3844
  53.2 8.2 %copy-start.9 = (s32[3200,1]{0,1:T(1,128)S(1)}, s32[3200,1]{0,1:T(1,128)}, u32[]{:S(2)}) copy-start(s32[3200,1]{0,1:T(1,128)} %param.10) | copy-start | bytes 38404
  53.2 126.9 %all-to-all-start = ((bf16[40,128,2,320]{1,0,2,3:T(8,128)(2,1)}), bf16[40,128,2,320]{1,0,2,3:T(8,128)(2,1)}, u32[]{:S(2)}, u32[]{:S(2)}) async-start(bf16[40,128,2,320]{1,0,2,3:T(8,128)(2,1)} %copy.122), calls=%async_computation | async-start | bytes 13107200 | tf_op jit(solution)/shard_map/all_to_all | solution.py:107
  61.0 6.8 copy-start.12
  61.0 6.8 copy-start.11
  180.1 4.8 copy-start.5
  180.1 4.9 copy-start.6
  245.7 75.4 %all-to-all-start.1 = ((bf16[16,400,128]{2,1,0:T(8,128)(2,1)}), bf16[16,400,128]{2,1,0:T(8,128)(2,1)}, u32[]{:S(2)}, u32[]{:S(2)}) async-start(bf16[16,400,128]{2,1,0:T(8,128)(2,1)} %bitcast.128), calls=%async_computation.1 | async-start | bytes 3276800 | tf_op jit(solution)/shard_map/all_to_all | solution.py:123
  313.9 7.2 copy-start.13
  321.0 24.3 %copy-start.14 = (bf16[1,1024,128]{2,1,0:T(8,128)(2,1)S(1)}, bf16[1,1024,128]{2,1,0:T(8,128)(2,1)}, u32[]{:S(2)}) copy-start(bf16[1,1024,128]{2,1,0:T(8,128)(2,1)} %param.13) | copy-start | bytes 786436
  358.3 48.7 %all-to-all-start.2 = ((bf16[16,400,128]{2,1,0:T(8,128)(2,1)}), bf16[16,400,128]{2,1,0:T(8,128)(2,1)S(1)}, u32[]{:S(2)}, u32[]{:S(2)}) async-start(bf16[16,400,128]{2,1,0:T(8,128)(2,1)} %bitcast.129), calls=%async_computation.2 | async-start | bytes 3276800 | tf_op jit(solution)/shard_map/all_to_all | solution.py:127
  380.0 27.0 %copy-start.2 = (s32[3200]{0:T(1024)S(1)}, s32[3200]{0:T(1024)}, u32[]{:S(2)}) copy-start(s32[3200]{0:T(1024)} %get-tuple-element.5) | copy-start | bytes 38404
  441.8 14.2 %copy-start.3 = (bf16[640,1,1280]{2,0,1:T(8,128)(2,1)S(1)}, bf16[640,1,1280]{2,0,1:T(8,128)(2,1)}, u32[]{:S(2)}) copy-start(bf16[640,1,1280]{2,0,1:T(8,128)(2,1)} %get-tuple-element.18) | copy-start | bytes 4915204
  441.8 14.2 %copy-start.4 = (bf16[640,1,1280]{2,0,1:T(8,128)(2,1)S(1)}, bf16[640,1,1280]{2,0,1:T(8,128)(2,1)}, u32[]{:S(2)}) copy-start(bf16[640,1,1280]{2,0,1:T(8,128)(2,1)} %get-tuple-element.20) | copy-start | bytes 4915204
  655.1 1.1 copy-start.8
  708.8 10.1 %copy-start.1 = (bf16[1,1024,1024]{2,1,0:T(8,128)(2,1)S(1)}, bf16[1,1024,1024]{2,1,0:T(8,128)(2,1)}, u32[]{:S(2)}) copy-start(bf16[1,1024,1024]{2,1,0:T(8,128)(2,1)} %param.12) | copy-start | bytes 6291460
where the time goes:
time: 726 us; the launch traced here: 719 us
  local copies, waits for them, and re-layouts  270 us (37%)
  blocking collectives  150 us (21%)
  waiting for transfers between devices  95.2 us (13%)
  matrix products  84.6 us (12%)
  other arithmetic  75.7 us (10%)
  starting transfers between devices  42.7 us (6%)
    all_to_all x1, blocking collectives, on_device(): lax.all_to_all(fourier_out, 'wave', split_axis=0, concat_axis=3, tiled=True)  150 us
    all_to_all x1, waiting for transfers between devices, on_device(): lax.all_to_all(fourier_in, 'wave', split_axis=3, concat_axis=0, tiled=True)  95.2 us
    convert_element_type x3, local copies, waits for them, and re-layouts, on_device(): spectral_out = result.astype(jnp.bfloat16)  47 us
    slice x6, local copies, waits for them, and re-layouts, forcing(): jnp.roll(flattened, -1, axis=0)  46.4 us
    convert_element_type x1, local copies, waits for them, and re-layouts, on_device(): fourier_out = jnp.einsum('fal,qrl->qfra', tendency_grid, forward_table, p...  38.3 us
    reshape x2, local copies, waits for them, and re-layouts, on_device(): inverse_out.astype(jnp.bfloat16)  30.7 us
    all_to_all x1, starting transfers between devices, on_device(): lax.all_to_all(outgoing, 'wave', split_axis=0, concat_axis=0, tiled=True)  28.9 us
    concatenate x1, local copies, waits for them, and re-layouts, forcing(): jnp.roll(flattened, -1, axis=0)  26.9 us
  transfers between devices with their start and end apart: 3, of which 1 were waited for; matrix products, arithmetic and copies ran while one was open for 16% of the time, Pallas kernels for 0%

commit v1 on v0

--- a/solution.py
+++ b/solution.py
@@ -1,12 +1,18 @@
+import functools
 import math
 
 import jax
 import jax.numpy as jnp
 from jax import lax
+from jax.experimental import pallas as pl
+from jax.experimental.pallas import tpu as pltpu
 from jax.sharding import PartitionSpec as P
 
 NLON = 1280
 FIELDS = 4
+PAIR_STEP = 4
+ROW_PARTS = 5
+SLOT_PARTS = 2
 
 
 def slot_waves(pair_low, wave_total):
@@ -88,7 +94,7 @@
     return jnp.sum(jnp.where(side_mask[:, :, :, None, None], both_sides, 0.0), axis=1)
 
 
-def on_device(spectral, legendre, pair_low, routes, w_in, w_mid, w_out):
+def on_device_arrays(spectral, legendre, pair_low, routes, w_in, w_mid, w_out):
     pair_count = spectral.shape[0]
     degrees = spectral.shape[1]
     channels = spectral.shape[2]
@@ -139,6 +145,366 @@
     return spectral_out.reshape(pair_count, degrees, channels)
 
 
+def cost(flops, moved):
+    return pl.CostEstimate(flops=int(flops), bytes_accessed=int(moved), transcendentals=0)
+
+
+def channel_order(channels):
+    source = jnp.arange(channels, dtype=jnp.int32)
+    target = source % 2 * (channels // 2) + source // 2
+    return (target[:, None] == source[None, :]).astype(jnp.bfloat16)
+
+
+def inverse_kernel(spans, devices, low_ref, spectral_ref, legendre_ref, order_ref, *rest):
+    outs, scratch = rest[:-1], rest[-1]
+    step = pl.program_id(0)
+    degrees, channels = spectral_ref.shape[1:]
+    lat_total = legendre_ref.shape[2]
+    rows = 2 * PAIR_STEP
+    degree = lax.broadcasted_iota(jnp.int32, (degrees, channels), 0)
+    for i in range(PAIR_STEP):
+        low = low_ref[step * PAIR_STEP + i]
+        ordered = jnp.dot(spectral_ref[i], order_ref[...], preferred_element_type=jnp.float32)
+        lower = degree < degrees - 1 - low
+        sides = jnp.concatenate(
+            [jnp.where(lower, ordered, 0.0), jnp.where(lower, 0.0, ordered)], axis=1
+        ).astype(jnp.bfloat16)
+        result = lax.dot_general(
+            legendre_ref[i], sides, (((0,), (0,)), ((), ())), preferred_element_type=jnp.float32
+        )
+        for s in range(2):
+            for h in range(channels // 128):
+                at = s * channels + h * 128
+                scratch[h, pl.ds(2 * i + s, lat_total, stride=rows), :] = result[:, at : at + 128]
+    per_device = lat_total // devices
+    for out, (first, count) in zip(outs, spans):
+        for d in range(devices):
+            for h in range(channels // 128):
+                block = scratch[h, pl.ds((d * per_device + first) * rows, count * rows), :]
+                out[d, :, :, h * 128 : (h + 1) * 128] = block.reshape(count, rows, 128).astype(
+                    jnp.bfloat16
+                )
+
+
+def inverse_legendre(spectral, legendre, local_low, order, spans, devices):
+    pair_count, degrees, channels = spectral.shape
+    lat_total = legendre.shape[2]
+    rows = 2 * PAIR_STEP
+    return pl.pallas_call(
+        functools.partial(inverse_kernel, spans, devices),
+        grid_spec=pltpu.PrefetchScalarGridSpec(
+            num_scalar_prefetch=1,
+            grid=(pair_count // PAIR_STEP,),
+            in_specs=[
+                pl.BlockSpec((PAIR_STEP, degrees, channels), lambda g, low: (g, 0, 0)),
+                pl.BlockSpec((PAIR_STEP, degrees, lat_total), lambda g, low: (g, 0, 0)),
+                pl.BlockSpec((channels, channels), lambda g, low: (0, 0)),
+            ],
+            out_specs=[
+                pl.BlockSpec((devices, count, rows, channels), lambda g, low: (0, 0, g, 0))
+                for _, count in spans
+            ],
+            scratch_shapes=[pltpu.VMEM((channels // 128, lat_total * rows, 128), jnp.float32)],
+        ),
+        out_shape=[
+            jax.ShapeDtypeStruct((devices, count, 2 * pair_count, channels), jnp.bfloat16)
+            for _, count in spans
+        ],
+        name="inverse_legendre",
+        cost_estimate=cost(
+            4 * pair_count * degrees * lat_total * channels, 2 * spectral.size * 2 + 2 * legendre.size
+        ),
+    )(local_low, spectral, legendre, order)
+
+
+def grid_kernel(coeff_ref, table_ref, forced_ref, columns_ref, pooled):
+    devices, lats, slots, channels = coeff_ref.shape
+    feat = channels // 2
+    rights = []
+    for t in range(lats):
+        waves = coeff_ref[:, t].astype(jnp.float32).reshape(devices * slots, channels)
+        rights.append(
+            jnp.concatenate([waves[:, :feat], waves[:, feat:]], axis=0).astype(jnp.bfloat16)
+        )
+    fields = jnp.dot(
+        table_ref[...], jnp.concatenate(rights, axis=1), preferred_element_type=jnp.float32
+    )
+    total = None
+    for t in range(lats):
+        one = fields[:, t * feat : (t + 1) * feat]
+        forced_ref[t] = one * pltpu.roll(one, feat - feat // 4, 1)
+        total = one if total is None else total + one
+    pooled[...] = total
+    count = columns_ref.shape[0]
+    spread = total.shape[0] // count
+    mean = pooled[pl.ds(0, count, stride=spread), :]
+    for u in range(1, spread):
+        mean = mean + pooled[pl.ds(u, count, stride=spread), :]
+    columns_ref[...] = (mean * (1.0 / (spread * lats))).astype(jnp.bfloat16)
+
+
+def to_grid(coeffs, table):
+    devices, lats, slots, channels = coeffs.shape
+    points = table.shape[0]
+    feat = channels // 2
+    return pl.pallas_call(
+        grid_kernel,
+        grid=(lats // 2,),
+        in_specs=[
+            pl.BlockSpec((devices, 2, slots, channels), lambda i: (0, i, 0, 0)),
+            pl.BlockSpec(table.shape, lambda i: (0, 0)),
+        ],
+        out_specs=[
+            pl.BlockSpec((2, points, feat), lambda i: (i, 0, 0)),
+            pl.BlockSpec((points // 4, feat), lambda i: (i, 0)),
+        ],
+        out_shape=[
+            jax.ShapeDtypeStruct((lats, points, feat), jnp.float32),
+            jax.ShapeDtypeStruct((lats // 2 * (points // 4), feat), jnp.bfloat16),
+        ],
+        scratch_shapes=[pltpu.VMEM((points, feat), jnp.float32)],
+        name="to_grid",
+        cost_estimate=cost(2 * coeffs.size * points, 2 * coeffs.size + 2 * table.size),
+    )(coeffs, table)
+
+
+def fourier_kernel(forced_ref, returned_ref, table_ref, out_ref, fine):
+    lats, points, feat = forced_ref.shape
+    devices, _, slots, _ = out_ref.shape
+    coarse = returned_ref[...].astype(jnp.float32)
+    count = coarse.shape[0]
+    before = pltpu.roll(coarse, 1, 0)
+    following = pltpu.roll(coarse, count - 1, 0)
+    pieces = [
+        0.375 * before + 0.625 * coarse,
+        0.125 * before + 0.875 * coarse,
+        0.875 * coarse + 0.125 * following,
+        0.625 * coarse + 0.375 * following,
+    ]
+    for u, piece in enumerate(pieces):
+        fine[pl.ds(u, count, stride=4), :] = piece
+    correction = fine[...]
+    right = jnp.concatenate(
+        [(forced_ref[t] + correction).astype(jnp.bfloat16) for t in range(lats)], axis=1
+    )
+    waves = jnp.dot(table_ref[...], right, preferred_element_type=jnp.float32)
+    half = devices * slots
+    for t in range(lats):
+        for r in range(2):
+            part = waves[r * half : (r + 1) * half, t * feat : (t + 1) * feat]
+            out_ref[:, t, :, r * feat : (r + 1) * feat] = part.reshape(devices, slots, feat).astype(
+                jnp.bfloat16
+            )
+
+
+def to_fourier(forced, returned, table, devices):
+    lats, points, feat = forced.shape
+    slots = table.shape[0] // (2 * devices)
+    return pl.pallas_call(
+        fourier_kernel,
+        grid=(lats // 2,),
+        in_specs=[
+            pl.BlockSpec((2, points, feat), lambda i: (i, 0, 0)),
+            pl.BlockSpec((points // 4, feat), lambda i: (i, 0)),
+            pl.BlockSpec(table.shape, lambda i: (0, 0)),
+        ],
+        out_specs=pl.BlockSpec((devices, 2, slots, 2 * feat), lambda i: (0, i, 0, 0)),
+        out_shape=jax.ShapeDtypeStruct((devices, lats, slots, 2 * feat), jnp.bfloat16),
+        scratch_shapes=[pltpu.VMEM((points, feat), jnp.float32)],
+        name="to_fourier",
+        cost_estimate=cost(2 * forced.size * table.shape[0], 4 * forced.size + 2 * table.size),
+    )(forced, returned, table)
+
+
+def forward_kernel(spans, low_ref, legendre_ref, order_ref, *rest):
+    coeffs, out_ref, scratch = rest[:-2], rest[-2], rest[-1]
+    step = pl.program_id(0)
+    _, degrees, channels = out_ref.shape
+    lat_total = legendre_ref.shape[2]
+    rows = 2 * PAIR_STEP
+    devices = coeffs[0].shape[0]
+    per_device = lat_total // devices
+    for ref, (first, count) in zip(coeffs, spans):
+        for d in range(devices):
+            block = ref[d].astype(jnp.float32).reshape(count * rows, channels)
+            for h in range(channels // 128):
+                scratch[h, pl.ds((d * per_device + first) * rows, count * rows), :] = block[
+                    :, h * 128 : (h + 1) * 128
+                ]
+    degree = lax.broadcasted_iota(jnp.int32, (degrees, channels), 0)
+    for i in range(PAIR_STEP):
+        low = low_ref[step * PAIR_STEP + i]
+        sides = []
+        for s in range(2):
+            side = jnp.concatenate(
+                [
+                    scratch[h, pl.ds(2 * i + s, lat_total, stride=rows), :]
+                    for h in range(channels // 128)
+                ],
+                axis=1,
+            ).astype(jnp.bfloat16)
+            sides.append(
+                lax.dot_general(
+                    side,
+                    order_ref[...],
+                    (((1,), (1,)), ((), ())),
+                    preferred_element_type=jnp.float32,
+                ).astype(jnp.bfloat16)
+            )
+        both = jnp.dot(
+            legendre_ref[i], jnp.concatenate(sides, axis=1), preferred_element_type=jnp.float32
+        )
+        lower = degree < degrees - 1 - low
+        out_ref[i] = jnp.where(lower, both[:, :channels], both[:, channels:]).astype(jnp.bfloat16)
+
+
+def forward_legendre(coeffs, legendre, local_low, order, spans):
+    pair_count, degrees, lat_total = legendre.shape
+    channels = order.shape[0]
+    rows = 2 * PAIR_STEP
+    devices = coeffs[0].shape[0]
+    return pl.pallas_call(
+        functools.partial(forward_kernel, spans),
+        grid_spec=pltpu.PrefetchScalarGridSpec(
+            num_scalar_prefetch=1,
+            grid=(pair_count // PAIR_STEP,),
+            in_specs=[
+                pl.BlockSpec((PAIR_STEP, degrees, lat_total), lambda g, low: (g, 0, 0)),
+                pl.BlockSpec((channels, channels), lambda g, low: (0, 0)),
+            ]
+            + [
+                pl.BlockSpec((devices, count, rows, channels), lambda g, low: (0, 0, g, 0))
+                for _, count in spans
+            ],
+            out_specs=pl.BlockSpec((PAIR_STEP, degrees, channels), lambda g, low: (g, 0, 0)),
+            scratch_shapes=[pltpu.VMEM((channels // 128, lat_total * rows, 128), jnp.float32)],
+        ),
+        out_shape=jax.ShapeDtypeStruct((pair_count, degrees, channels), jnp.bfloat16),
+        name="forward_legendre",
+        cost_estimate=cost(
+            4 * pair_count * degrees * lat_total * channels, 4 * legendre.size
+        ),
+    )(local_low, legendre, order, *coeffs)
+
+
+def smooth(values):
+    half = 0.5 * values
+    return half + half * jnp.tanh(half)
+
+
+def network_kernel(rows_ref, in_ref, mid_ref, out_w_ref, out_ref):
+    sources, slots, feat = rows_ref.shape
+    rows = rows_ref[...].reshape(sources * slots, feat)
+    hidden = smooth(jnp.dot(rows, in_ref[0], preferred_element_type=jnp.float32))
+    deeper = smooth(
+        jnp.dot(hidden.astype(jnp.bfloat16), mid_ref[0], preferred_element_type=jnp.float32)
+    )
+    answer = jnp.dot(
+        deeper.astype(jnp.bfloat16), out_w_ref[0], preferred_element_type=jnp.float32
+    )
+    out_ref[...] = answer.reshape(sources, slots, feat).astype(jnp.bfloat16)
+
+
+def run_network(arrived, w_in, w_mid, w_out):
+    devices, slots, feat = arrived.shape
+    group = math.gcd(devices, 4)
+    return pl.pallas_call(
+        network_kernel,
+        grid=(devices // group,),
+        in_specs=[
+            pl.BlockSpec((group, slots, feat), lambda i: (i, 0, 0)),
+            pl.BlockSpec(w_in.shape, lambda i: (0, 0, 0)),
+            pl.BlockSpec(w_mid.shape, lambda i: (0, 0, 0)),
+            pl.BlockSpec(w_out.shape, lambda i: (0, 0, 0)),
+        ],
+        out_specs=pl.BlockSpec((group, slots, feat), lambda i: (i, 0, 0)),
+        out_shape=jax.ShapeDtypeStruct(arrived.shape, jnp.bfloat16),
+        name="network",
+        cost_estimate=cost(
+            2 * devices * slots * (w_in.size + w_mid.size + w_out.size), 4 * arrived.size + 2 * w_mid.size
+        ),
+    )(arrived, w_in, w_mid, w_out)
+
+
+def phase_tables(wavenums, points):
+    longitude = jnp.arange(points, dtype=jnp.int32)
+    turn = jnp.float32(2.0 * math.pi / points)
+    angles = (wavenums[:, None] * longitude[None, :] % points).astype(jnp.float32) * turn
+    scale = jnp.float32(1.0 / math.sqrt(points))
+    forward = jnp.concatenate([scale * jnp.cos(angles), -scale * jnp.sin(angles)], axis=0).astype(
+        jnp.bfloat16
+    )
+    angles = (longitude[:, None] * wavenums[None, :] % points).astype(jnp.float32) * turn
+    factor = jnp.where(wavenums == 0, jnp.float32(1.0), jnp.float32(2.0))[None, :]
+    inverse = jnp.concatenate([factor * jnp.cos(angles), -factor * jnp.sin(angles)], axis=1).astype(
+        jnp.bfloat16
+    )
+    return inverse, forward
+
+
+def exchange(values):
+    return lax.all_to_all(values, "wave", split_axis=0, concat_axis=0, tiled=True)
+
+
+def row_spans(lat_rows):
+    pairs = lat_rows // 2
+    parts = math.gcd(pairs, ROW_PARTS)
+    count = pairs // parts * 2
+    return [(part * count, count) for part in range(parts)]
+
+
+def on_device_kernels(spectral, legendre, pair_low, routes, w_in, w_mid, w_out):
+    pair_count, degrees, channels = spectral.shape
+    feat = channels // 2
+    lat_total = legendre.shape[2]
+    wave_total = degrees - 1
+    devices = lax.axis_size("wave")
+    lat_rows = lat_total // devices
+    spans = row_spans(lat_rows)
+    local_low = lax.dynamic_slice_in_dim(pair_low, lax.axis_index("wave") * pair_count, pair_count)
+    order = channel_order(channels)
+    sent = inverse_legendre(spectral, legendre, local_low, order, spans, devices)
+    inverse_table, forward_table = phase_tables(slot_waves(pair_low, wave_total), NLON)
+    regimes = routes[:, 0]
+    total_columns = regimes.shape[0]
+    positions = slot_positions(regimes.reshape(1, -1), devices)[0]
+    capacity = 2 * total_columns // devices
+    slots = capacity // SLOT_PARTS
+    places = (positions // slots * devices + regimes) * slots + positions % slots
+    outgoing = jnp.zeros((SLOT_PARTS * devices * slots, feat), jnp.bfloat16)
+    forced = []
+    width = NLON // 4
+    for part, (first, count) in zip(sent, spans):
+        forced_part, columns = to_grid(exchange(part), inverse_table)
+        forced.append(forced_part)
+        at = places[first // 2 * width : (first + count) // 2 * width]
+        outgoing = outgoing.at[at].set(columns, unique_indices=True, mode="promise_in_bounds")
+    outgoing = outgoing.reshape(SLOT_PARTS, devices, slots, feat)
+    answers = [
+        exchange(run_network(exchange(outgoing[part]), w_in, w_mid, w_out))
+        for part in range(SLOT_PARTS)
+    ]
+    incoming = jnp.concatenate(answers, axis=0).reshape(-1, feat)
+    received = []
+    for forced_part, (first, count) in zip(forced, spans):
+        at = places[first // 2 * width : (first + count) // 2 * width]
+        returned = incoming.at[at].get(mode="promise_in_bounds")
+        received.append(exchange(to_fourier(forced_part, returned, forward_table, devices)))
+    return forward_legendre(received, legendre, local_low, order, spans)
+
+
+def on_device(spectral, legendre, pair_low, routes, w_in, w_mid, w_out):
+    devices = lax.axis_size("wave")
+    aligned = (
+        spectral.shape[0] % PAIR_STEP == 0
+        and 2 * spectral.shape[0] % 8 == 0
+        and legendre.shape[2] // devices % 2 == 0
+        and 2 * routes.shape[0] // devices % (8 * SLOT_PARTS) == 0
+    )
+    body = on_device_kernels if aligned else on_device_arrays
+    return body(spectral, legendre, pair_low, routes, w_in, w_mid, w_out)
+
+
 def solution(mesh):
     placed = (
         P(("grp", "wave"), None, None),

time: 726 us -> 566 us (0.78)
  local copies, waits for them, and re-layouts: 270 us -> 56.9 us
  Pallas kernels: 0 us -> 116 us
  matrix products: 84.6 us -> 0 us
  other arithmetic: 75.7 us -> 38.7 us
  blocking collectives: 150 us -> 177 us
  waiting for transfers between devices: 95.2 us -> 113 us
  starting transfers between devices: 42.7 us -> 54.2 us
    pallas_call x0 -> x14, Pallas kernels: none -> 116 us  [the longest x2 28.6 us: run_network(): pl.pallas_call(network_kernel, grid=(devices // group,), in_specs=[pl.Blo...]
    convert_element_type x5 -> x0, local copies, waits for them, and re-layouts: 95.1 us -> none  [the longest x3 47 us: on_device(): spectral_out = result.astype(jnp.bfloat16)]
    dot_general x6 -> x0, matrix products: 84.6 us -> none  [the longest x1 24.3 us: network(): jnp.dot(hidden, weight_mid, preferred_element_type=jnp.float32)]
    slice x6 -> x2, local copies, waits for them, and re-layouts: 46.4 us -> 1.45 us  [the longest x1 1 us: on_device_kernels(): outgoing[part]]
    reshape x3 -> x1, local copies, waits for them, and re-layouts: 38.8 us -> 0.14 us  [slot_waves(): return jnp.stack([pair_low, wave_total - 1 - pair_low], axis=1).reshape(-1)]
    scatter x0 -> x5, local copies, waits for them, and re-layouts: none -> 27.7 us  [on_device_kernels(): outgoing.at[at].set(columns, unique_indices=True, mode='promise_in_bounds')]
    concatenate x3 -> x0, local copies, waits for them, and re-layouts: 27.3 us -> none  [the longest x1 26.9 us: forcing(): jnp.roll(flattened, -1, axis=0)]
    all_to_all x1 -> x5, blocking collectives: 150 us -> 177 us  [exchange(): lax.all_to_all(values, 'wave', split_axis=0, concat_axis=0, tiled=True)]
  transfers between devices with their start and end apart: 3 -> 9, of which waited for: 1 -> 8; matrix products, arithmetic and copies ran while one was open for 16% -> 13% of each run, Pallas kernels for 0% -> 13%
where the time goes in v1:
time: 566 us; the launch traced here: 556 us
  blocking collectives  177 us (31%)
  Pallas kernels  116 us (20%)
  waiting for transfers between devices  113 us (20%)
  local copies, waits for them, and re-layouts  56.9 us (10%)
  starting transfers between devices  54.2 us (10%)
  other arithmetic  38.7 us (7%)
    all_to_all x5, blocking collectives, exchange(): lax.all_to_all(values, 'wave', split_axis=0, concat_axis=0, tiled=True)  177 us
    all_to_all x9, waiting for transfers between devices, exchange(): lax.all_to_all(values, 'wave', split_axis=0, concat_axis=0, tiled=True)  113 us
    all_to_all x9, starting transfers between devices, exchange(): lax.all_to_all(values, 'wave', split_axis=0, concat_axis=0, tiled=True)  54.2 us
    another operation x5, other arithmetic  33.8 us
    pallas_call x2, Pallas kernels, run_network(): pl.pallas_call(network_kernel, grid=(devices // group,), in_specs=[pl.Blo...  28.6 us
    scatter x5, local copies, waits for them, and re-layouts, on_device_kernels(): outgoing.at[at].set(columns, unique_indices=True, mode='promise_in_bounds')  27.7 us
    pallas_call x5, Pallas kernels, to_grid(): pl.pallas_call(grid_kernel, grid=(lats // 2,), in_specs=[pl.BlockSpec((de...  27.5 us
    pallas_call x5, Pallas kernels, to_fourier(): pl.pallas_call(fourier_kernel, grid=(lats // 2,), in_specs=[pl.BlockSpec(...  27.4 us
  transfers between devices with their start and end apart: 9, of which 8 were waited for; matrix products, arithmetic and copies ran while one was open for 13% of the time, Pallas kernels for 13%

profile of v1, /device:TPU:1, one launch (start us, length us, event | category | flops | bytes accessed | tf_op | source)
XLA Modules:
  0.0 556.4 jit_solution(18067885222467723817)
XLA Ops:
  0.0 14.0 %copy.12.legendre_ref = bf16[20,641,320]{2,1,0:T(8,128)(2,1)} copy(bf16[20,641,320]{1,2,0:T(8,128)(2,1)} %param.8) | data formatting | bytes 16409600 | tf_op args[1]
  14.0 0.8 fusion.12.order_ref
  14.8 0.0 copy-done.7
  14.8 0.6 dynamic_slice.3.low_ref
  15.4 15.5 %inverse_legendre.1 = (bf16[16,4,40,256]{3,2,1,0:T(8,128)(2,1)}, bf16[16,4,40,256]{3,2,1,0:T(8,128)(2,1)}, bf16[16,4,40,256]{3,2,1,0:T(8,128)(2,1)}, bf16[16,4,4...) custom-call(s32[20]{0:T(128)} %dynamic_slice.3.low_ref, bf16[20,641,256]{2,1,0:T(8,128)(2,1)} %spectral_ref.1, ...), custom_call_target="tpu_custom_call" | custom-call | flops 4200857600 | bytes 21332480 | tf_op jit(solution)/shard_map/inverse_legendre/pallas_call | solution.py:193
  30.9 39.4 %all_to_all.70.coeff_ref = bf16[16,4,40,256]{3,2,1,0:T(8,128)(2,1)} all-to-all(bf16[16,4,40,256]{3,2,1,0:T(8,128)(2,1)} %get-tuple-element.20), channel_id=1, replica_groups=mesh['grp'=2,'wave'=16] {'wave'}, dimensions={0} | all-to-all | bytes 2621440 | tf_op jit(solution)/shard_map/all_to_all | solution.py:446
  70.3 35.4 %all_to_all.71.coeff_ref = bf16[16,4,40,256]{3,2,1,0:T(8,128)(2,1)} all-to-all(bf16[16,4,40,256]{3,2,1,0:T(8,128)(2,1)S(1)} %copy-done.4), channel_id=1, replica_groups=mesh['grp'=2,'wave'=16] {'wave'}, dimensions={0} | all-to-all | bytes 2621440 | tf_op jit(solution)/shard_map/all_to_all | solution.py:446
  105.7 35.3 %all_to_all.72.coeff_ref = bf16[16,4,40,256]{3,2,1,0:T(8,128)(2,1)} all-to-all(bf16[16,4,40,256]{3,2,1,0:T(8,128)(2,1)S(1)} %copy-done.3), channel_id=1, replica_groups=mesh['grp'=2,'wave'=16] {'wave'}, dimensions={0} | all-to-all | bytes 2621440 | tf_op jit(solution)/shard_map/all_to_all | solution.py:446
  141.0 3.7 all-to-all-start.3
  144.8 0.1 copy.11
  144.9 0.1 reshape.163
  145.2 4.6 reduce-window.6
  149.9 0.5 slice_reduce_fusion
  150.3 0.2 reduce-window.9
  150.5 0.1 broadcast.147
  150.7 21.8 %all-to-all-done.3.coeff_ref = bf16[16,4,40,256]{3,2,1,0:T(8,128)(2,1)S(1)} async-done(((bf16[16,4,40,256]{3,2,1,0:T(8,128)(2,1)}), bf16[16,4,40,256]{3,2,1,0:T(8,128)(2,1)S(1)}, u32[]{:S(2)}, u32[]{:S(2)}) %all-to-all-start.3) | async-done | bytes 1310752 | tf_op jit(solution)/shard_map/all_to_all | solution.py:446
  172.5 7.5 %all-to-all-start.4 = ((bf16[16,4,40,256]{3,2,1,0:T(8,128)(2,1)}), bf16[16,4,40,256]{3,2,1,0:T(8,128)(2,1)}, u32[]{:S(2)}, u32[]{:S(2)}) async-start(bf16[16,4,40,256]{3,2,1,0:T(8,128)(2,1)} %get-tuple-element.29), calls=%async_computation.4 | async-start | bytes 2621440 | tf_op jit(solution)/shard_map/all_to_all | solution.py:446
  179.9 0.1 fusion.13
  180.0 13.9 %multiply_convert_fusion.3 = (bf16[1280,640]{1,0:T(8,128)(2,1)S(1)}, bf16[1280,640]{1,0:T(8,128)(2,1)S(1)}) fusion(s32[640]{0:T(1024)S(1)} %reshape.163, f32[640]{0:T(1024)S(1)} %get-tuple-element.46, f32[640]{0:T(1024)S(1)} %get-tuple-element.47), kind=kLoop, calls=%fused_computation.24 | loop fusion | flops 10649600 | bytes 3284480 | tf_op jit(solution)/shard_map/convert.4
  194.0 1.9 pad_maximum_fusion.table_ref
  195.9 5.5 to_grid.5
  201.4 5.2 scatter_custom_fusion
  206.6 5.5 to_grid.6
  212.1 5.7 %scatter_fusion = bf16[6400,128]{1,0:T(8,128)(2,1)S(1)} fusion(bf16[6400,128]{1,0:T(8,128)(2,1)S(1)} %scatter_custom_fusion, s32[640]{0:T(1024)S(1)} %get-tuple-element.40, bf16[640,128]{1,0:T(8,128)(2,1)} %get-tuple-element.24), kind=kCustom, calls=%fused_computation.6 | custom fusion | bytes 494080 | tf_op jit(solution)/shard_map/scatter | solution.py:481
  217.8 5.5 to_grid.7
  223.3 5.5 scatter_fusion.1
  228.9 5.5 to_grid.8
  234.4 5.5 scatter_fusion.2
  239.9 0.0 all-to-all-done.4.coeff_ref
  239.9 5.5 to_grid.9
  245.4 5.7 %scatter_fusion.3 = bf16[6400,128]{1,0:T(8,128)(2,1)S(1)} fusion(bf16[6400,128]{1,0:T(8,128)(2,1)S(1)} %scatter_fusion.2, s32[640]{0:T(1024)S(1)} %get-tuple-element.37, bf16[640,128]{1,0:T(8,128)(2,1)} %get-tuple-element.30), kind=kCustom, calls=%fused_computation.9 | custom fusion | bytes 494080 | tf_op jit(solution)/shard_map/scatter | solution.py:481
  251.2 1.0 fusion.24
  252.2 27.2 %all_to_all.73.rows_ref = bf16[16,200,128]{2,1,0:T(8,128)(2,1)} all-to-all(bf16[16,200,128]{2,1,0:T(8,128)(2,1)S(1)} %bitcast.17), channel_id=1, replica_groups=mesh['grp'=2,'wave'=16] {'wave'}, dimensions={0} | all-to-all | bytes 1638400 | tf_op jit(solution)/shard_map/all_to_all | solution.py:446
  279.4 3.5 all-to-all-start.7
  282.9 14.3 %network.2 = bf16[16,200,128]{2,1,0:T(8,128)(2,1)} custom-call(bf16[16,200,128]{2,1,0:T(8,128)(2,1)} %all_to_all.73.rows_ref, bf16[1,128,1024]{2,1,0:T(8,128)(2,1)} %in_ref.3, bf16[1,1024,1024]{2,1,0:T(8,128)(2,1)} %mid_ref.3, bf16[1,1024,128]{2,1,0:T(8,128)(2,1)} %out_w_ref.3), custom_call_target="tpu_custom_call" | custom-call | flops 8388608000 | bytes 3735552 | tf_op jit(solution)/shard_map/network/pallas_call | solution.py:411
  297.2 4.9 all-to-all-done.7.rows_ref
  302.1 5.6 %all-to-all-start.6 = ((bf16[16,200,128]{2,1,0:T(8,128)(2,1)}), bf16[16,200,128]{2,1,0:T(8,128)(2,1)S(1)}, u32[]{:S(2)}, u32[]{:S(2)}) async-start(bf16[16,200,128]{2,1,0:T(8,128)(2,1)} %network.2), calls=%async_computation.6 | async-start | bytes 1638400 | tf_op jit(solution)/shard_map/all_to_all | solution.py:446
  307.6 14.3 %network.3 = bf16[16,200,128]{2,1,0:T(8,128)(2,1)} custom-call(bf16[16,200,128]{2,1,0:T(8,128)(2,1)} %copy-done.5, bf16[1,128,1024]{2,1,0:T(8,128)(2,1)} %in_ref.3, bf16[1,1024,1024]{2,1,0:T(8,128)(2,1)} %mid_ref.3, bf16[1,1024,128]{2,1,0:T(8,128)(2,1)} %out_w_ref.3), custom_call_target="tpu_custom_call" | custom-call | flops 8388608000 | bytes 3735552 | tf_op jit(solution)/shard_map/network/pallas_call | solution.py:411
  321.9 4.9 all-to-all-done.6
  326.8 5.9 %all-to-all-start.8 = ((bf16[16,200,128]{2,1,0:T(8,128)(2,1)}), bf16[16,200,128]{2,1,0:T(8,128)(2,1)S(1)}, u32[]{:S(2)}, u32[]{:S(2)}) async-start(bf16[16,200,128]{2,1,0:T(8,128)(2,1)} %network.3), calls=%async_computation.8 | async-start | bytes 1638400 | tf_op jit(solution)/shard_map/all_to_all | solution.py:446
  332.8 15.0 %multiply_convert_fusion.1 = (bf16[640,1280]{1,0:T(8,128)(2,1)S(1)}, bf16[640,1280]{1,0:T(8,128)(2,1)S(1)}) fusion(s32[640]{0:T(1024)S(1)} %reshape.163), kind=kLoop, calls=%fused_computation.19 | loop fusion | flops 10649600 | bytes 3279360 | tf_op jit(solution)/shard_map/convert.2
  347.8 1.9 pad_maximum_fusion.1.table_ref
  349.7 2.1 all-to-all-done.8
  351.8 0.1 pad_maximum_fusion.2
  352.0 2.5 gather_fusion.4
  354.5 5.5 to_fourier.9
  359.9 5.6 %all-to-all-start.13 = ((bf16[16,4,40,256]{3,2,1,0:T(8,128)(2,1)}), bf16[16,4,40,256]{3,2,1,0:T(8,128)(2,1)S(1)}, u32[]{:S(2)}, u32[]{:S(2)}) async-start(bf16[16,4,40,256]{3,2,1,0:T(8,128)(2,1)} %to_fourier.9), calls=%async_computation.13 | async-start | bytes 2621440 | tf_op jit(solution)/shard_map/all_to_all | solution.py:446
  365.5 2.5 gather_fusion.3
  368.0 5.5 to_fourier.8
  373.5 19.8 %all-to-all-done.13.rest_4_ = bf16[16,4,40,256]{3,2,1,0:T(8,128)(2,1)S(1)} async-done(((bf16[16,4,40,256]{3,2,1,0:T(8,128)(2,1)}), bf16[16,4,40,256]{3,2,1,0:T(8,128)(2,1)S(1)}, u32[]{:S(2)}, u32[]{:S(2)}) %all-to-all-start.13) | async-done | bytes 1310752 | tf_op jit(solution)/shard_map/all_to_all | solution.py:446
  393.4 7.5 %all-to-all-start.12 = ((bf16[16,4,40,256]{3,2,1,0:T(8,128)(2,1)}), bf16[16,4,40,256]{3,2,1,0:T(8,128)(2,1)}, u32[]{:S(2)}, u32[]{:S(2)}) async-start(bf16[16,4,40,256]{3,2,1,0:T(8,128)(2,1)} %to_fourier.8), calls=%async_computation.12 | async-start | bytes 2621440 | tf_op jit(solution)/shard_map/all_to_all | solution.py:446
  400.8 2.5 gather_fusion.2
  403.3 5.5 to_fourier.7
  408.8 20.0 %all-to-all-done.12.rest_3_ = bf16[16,4,40,256]{3,2,1,0:T(8,128)(2,1)} async-done(((bf16[16,4,40,256]{3,2,1,0:T(8,128)(2,1)}), bf16[16,4,40,256]{3,2,1,0:T(8,128)(2,1)}, u32[]{:S(2)}, u32[]{:S(2)}) %all-to-all-start.12) | async-done | bytes 1310752 | tf_op jit(solution)/shard_map/all_to_all | solution.py:446
  428.8 7.5 %all-to-all-start.11 = ((bf16[16,4,40,256]{3,2,1,0:T(8,128)(2,1)}), bf16[16,4,40,256]{3,2,1,0:T(8,128)(2,1)S(1)}, u32[]{:S(2)}, u32[]{:S(2)}) async-start(bf16[16,4,40,256]{3,2,1,0:T(8,128)(2,1)} %to_fourier.7), calls=%async_computation.11 | async-start | bytes 2621440 | tf_op jit(solution)/shard_map/all_to_all | solution.py:446
  436.2 2.5 gather_fusion.1
  438.8 5.5 to_fourier.6
  444.2 19.8 %all-to-all-done.11.rest_2_ = bf16[16,4,40,256]{3,2,1,0:T(8,128)(2,1)S(1)} async-done(((bf16[16,4,40,256]{3,2,1,0:T(8,128)(2,1)}), bf16[16,4,40,256]{3,2,1,0:T(8,128)(2,1)S(1)}, u32[]{:S(2)}, u32[]{:S(2)}) %all-to-all-start.11) | async-done | bytes 1310752 | tf_op jit(solution)/shard_map/all_to_all | solution.py:446
  464.1 7.5 %all-to-all-start.10 = ((bf16[16,4,40,256]{3,2,1,0:T(8,128)(2,1)}), bf16[16,4,40,256]{3,2,1,0:T(8,128)(2,1)}, u32[]{:S(2)}, u32[]{:S(2)}) async-start(bf16[16,4,40,256]{3,2,1,0:T(8,128)(2,1)} %to_fourier.6), calls=%async_computation.10 | async-start | bytes 2621440 | tf_op jit(solution)/shard_map/all_to_all | solution.py:446
  471.5 2.5 gather_fusion
  474.1 5.5 to_fourier.5
  479.5 19.9 %all-to-all-done.10.rest_1_ = bf16[16,4,40,256]{3,2,1,0:T(8,128)(2,1)} async-done(((bf16[16,4,40,256]{3,2,1,0:T(8,128)(2,1)}), bf16[16,4,40,256]{3,2,1,0:T(8,128)(2,1)}, u32[]{:S(2)}, u32[]{:S(2)}) %all-to-all-start.10) | async-done | bytes 1310752 | tf_op jit(solution)/shard_map/all_to_all | solution.py:446
  499.5 39.4 %all_to_all.74.rest_0_ = bf16[16,4,40,256]{3,2,1,0:T(8,128)(2,1)} all-to-all(bf16[16,4,40,256]{3,2,1,0:T(8,128)(2,1)} %to_fourier.5), channel_id=1, replica_groups=mesh['grp'=2,'wave'=16] {'wave'}, dimensions={0} | all-to-all | bytes 2621440 | tf_op jit(solution)/shard_map/all_to_all | solution.py:446
  538.9 17.1 %forward_legendre.1 = bf16[20,641,256]{2,1,0:T(8,128)(2,1)} custom-call(s32[20]{0:T(128)} %dynamic_slice.3.low_ref, bf16[20,641,320]{2,1,0:T(8,128)(2,1)} %copy.12.legendre_ref, bf16[256,256]{1,0:T(8,128)(2,1)} %fusion.12.order_ref, bf16[16,4,40,256]{3,2,1,0:T(8,128)(2,1)} %all_to_all.74.rest_0_, bf16[16,4,40,256]{3,2,1,0:T(8,128)(2,1)} %all-to-all-done.10.rest_1_, ...), custom_call_target="tpu_custom_call" | custom-call | flops 4200857600 | bytes 16409600 | tf_op jit(solution)/shard_map/forward_legendre/pallas_call | solution.py:366
  (34 shorter events, 0.3 us)
Async XLA Ops:
  0.0 14.8 %copy-start.7 = (s32[320]{0:T(512)S(1)}, s32[320]{0:T(512)}, u32[]{:S(2)}) copy-start(s32[320]{0:T(512)} %param.9) | copy-start | bytes 3844
  30.9 39.4 %copy-start.4 = (bf16[16,4,40,256]{3,2,1,0:T(8,128)(2,1)S(1)}, bf16[16,4,40,256]{3,2,1,0:T(8,128)(2,1)}, u32[]{:S(2)}) copy-start(bf16[16,4,40,256]{3,2,1,0:T(8,128)(2,1)} %get-tuple-element.23) | copy-start | bytes 3932164
  70.3 35.4 %copy-start.3 = (bf16[16,4,40,256]{3,2,1,0:T(8,128)(2,1)S(1)}, bf16[16,4,40,256]{3,2,1,0:T(8,128)(2,1)}, u32[]{:S(2)}) copy-start(bf16[16,4,40,256]{3,2,1,0:T(8,128)(2,1)} %get-tuple-element.25) | copy-start | bytes 3932164
  141.0 4.1 copy-start.6
  141.0 31.5 %all-to-all-start.3 = ((bf16[16,4,40,256]{3,2,1,0:T(8,128)(2,1)}), bf16[16,4,40,256]{3,2,1,0:T(8,128)(2,1)S(1)}, u32[]{:S(2)}, u32[]{:S(2)}) async-start(bf16[16,4,40,256]{3,2,1,0:T(8,128)(2,1)} %get-tuple-element.27), calls=%async_computation.3 | async-start | bytes 2621440 | tf_op jit(solution)/shard_map/all_to_all | solution.py:446
  172.5 21.5 %copy-start.2 = (bf16[16,4,40,256]{3,2,1,0:T(8,128)(2,1)}, bf16[16,4,40,256]{3,2,1,0:T(8,128)(2,1)S(1)}, u32[]{:S(2)}) copy-start(bf16[16,4,40,256]{3,2,1,0:T(8,128)(2,1)S(1)} %all-to-all-done.3.coeff_ref) | copy-start | bytes 3932164
  172.5 67.5 %all-to-all-start.4 = ((bf16[16,4,40,256]{3,2,1,0:T(8,128)(2,1)}), bf16[16,4,40,256]{3,2,1,0:T(8,128)(2,1)}, u32[]{:S(2)}, u32[]{:S(2)}) async-start(bf16[16,4,40,256]{3,2,1,0:T(8,128)(2,1)} %get-tuple-element.29), calls=%async_computation.4 | async-start | bytes 2621440 | tf_op jit(solution)/shard_map/all_to_all | solution.py:446
  279.4 22.7 %all-to-all-start.7 = ((bf16[16,200,128]{2,1,0:T(8,128)(2,1)}), bf16[16,200,128]{2,1,0:T(8,128)(2,1)S(1)}, u32[]{:S(2)}, u32[]{:S(2)}) async-start(bf16[16,200,128]{2,1,0:T(8,128)(2,1)} %bitcast.4), calls=%async_computation.7 | async-start | bytes 1638400 | tf_op jit(solution)/shard_map/all_to_all | solution.py:446
  302.1 5.6 %copy-start.5 = (bf16[16,200,128]{2,1,0:T(8,128)(2,1)}, bf16[16,200,128]{2,1,0:T(8,128)(2,1)S(1)}, u32[]{:S(2)}) copy-start(bf16[16,200,128]{2,1,0:T(8,128)(2,1)S(1)} %all-to-all-done.7.rows_ref) | copy-start | bytes 2457604
  302.1 24.8 %all-to-all-start.6 = ((bf16[16,200,128]{2,1,0:T(8,128)(2,1)}), bf16[16,200,128]{2,1,0:T(8,128)(2,1)S(1)}, u32[]{:S(2)}, u32[]{:S(2)}) async-start(bf16[16,200,128]{2,1,0:T(8,128)(2,1)} %network.2), calls=%async_computation.6 | async-start | bytes 1638400 | tf_op jit(solution)/shard_map/all_to_all | solution.py:446
  326.8 25.0 %all-to-all-start.8 = ((bf16[16,200,128]{2,1,0:T(8,128)(2,1)}), bf16[16,200,128]{2,1,0:T(8,128)(2,1)S(1)}, u32[]{:S(2)}, u32[]{:S(2)}) async-start(bf16[16,200,128]{2,1,0:T(8,128)(2,1)} %network.3), calls=%async_computation.8 | async-start | bytes 1638400 | tf_op jit(solution)/shard_map/all_to_all | solution.py:446
  359.9 33.4 %all-to-all-start.13 = ((bf16[16,4,40,256]{3,2,1,0:T(8,128)(2,1)}), bf16[16,4,40,256]{3,2,1,0:T(8,128)(2,1)S(1)}, u32[]{:S(2)}, u32[]{:S(2)}) async-start(bf16[16,4,40,256]{3,2,1,0:T(8,128)(2,1)} %to_fourier.9), calls=%async_computation.13 | async-start | bytes 2621440 | tf_op jit(solution)/shard_map/all_to_all | solution.py:446
  393.3 10.0 %copy-start = (bf16[16,4,40,256]{3,2,1,0:T(8,128)(2,1)}, bf16[16,4,40,256]{3,2,1,0:T(8,128)(2,1)S(1)}, u32[]{:S(2)}) copy-start(bf16[16,4,40,256]{3,2,1,0:T(8,128)(2,1)S(1)} %all-to-all-done.13.rest_4_) | copy-start | bytes 3932164
  393.4 35.4 %all-to-all-start.12 = ((bf16[16,4,40,256]{3,2,1,0:T(8,128)(2,1)}), bf16[16,4,40,256]{3,2,1,0:T(8,128)(2,1)}, u32[]{:S(2)}, u32[]{:S(2)}) async-start(bf16[16,4,40,256]{3,2,1,0:T(8,128)(2,1)} %to_fourier.8), calls=%async_computation.12 | async-start | bytes 2621440 | tf_op jit(solution)/shard_map/all_to_all | solution.py:446
  428.8 35.3 %all-to-all-start.11 = ((bf16[16,4,40,256]{3,2,1,0:T(8,128)(2,1)}), bf16[16,4,40,256]{3,2,1,0:T(8,128)(2,1)S(1)}, u32[]{:S(2)}, u32[]{:S(2)}) async-start(bf16[16,4,40,256]{3,2,1,0:T(8,128)(2,1)} %to_fourier.7), calls=%async_computation.11 | async-start | bytes 2621440 | tf_op jit(solution)/shard_map/all_to_all | solution.py:446
  464.1 10.0 %copy-start.1 = (bf16[16,4,40,256]{3,2,1,0:T(8,128)(2,1)}, bf16[16,4,40,256]{3,2,1,0:T(8,128)(2,1)S(1)}, u32[]{:S(2)}) copy-start(bf16[16,4,40,256]{3,2,1,0:T(8,128)(2,1)S(1)} %all-to-all-done.11.rest_2_) | copy-start | bytes 3932164
  464.1 35.4 %all-to-all-start.10 = ((bf16[16,4,40,256]{3,2,1,0:T(8,128)(2,1)}), bf16[16,4,40,256]{3,2,1,0:T(8,128)(2,1)}, u32[]{:S(2)}, u32[]{:S(2)}) async-start(bf16[16,4,40,256]{3,2,1,0:T(8,128)(2,1)} %to_fourier.6), calls=%async_computation.10 | async-start | bytes 2621440 | tf_op jit(solution)/shard_map/all_to_all | solution.py:446

commit v2 on v1

--- a/solution.py
+++ b/solution.py
@@ -11,7 +11,6 @@
 NLON = 1280
 FIELDS = 4
 PAIR_STEP = 4
-ROW_PARTS = 5
 SLOT_PARTS = 2
 
 
@@ -159,7 +158,7 @@
     outs, scratch = rest[:-1], rest[-1]
     step = pl.program_id(0)
     degrees, channels = spectral_ref.shape[1:]
-    lat_total = legendre_ref.shape[2]
+    lat_total = legendre_ref.shape[1]
     rows = 2 * PAIR_STEP
     degree = lax.broadcasted_iota(jnp.int32, (degrees, channels), 0)
     for i in range(PAIR_STEP):
@@ -169,9 +168,7 @@
         sides = jnp.concatenate(
             [jnp.where(lower, ordered, 0.0), jnp.where(lower, 0.0, ordered)], axis=1
         ).astype(jnp.bfloat16)
-        result = lax.dot_general(
-            legendre_ref[i], sides, (((0,), (0,)), ((), ())), preferred_element_type=jnp.float32
-        )
+        result = jnp.dot(legendre_ref[i], sides, preferred_element_type=jnp.float32)
         for s in range(2):
             for h in range(channels // 128):
                 at = s * channels + h * 128
@@ -188,7 +185,7 @@
 
 def inverse_legendre(spectral, legendre, local_low, order, spans, devices):
     pair_count, degrees, channels = spectral.shape
-    lat_total = legendre.shape[2]
+    lat_total = legendre.shape[1]
     rows = 2 * PAIR_STEP
     return pl.pallas_call(
         functools.partial(inverse_kernel, spans, devices),
@@ -197,7 +194,7 @@
             grid=(pair_count // PAIR_STEP,),
             in_specs=[
                 pl.BlockSpec((PAIR_STEP, degrees, channels), lambda g, low: (g, 0, 0)),
-                pl.BlockSpec((PAIR_STEP, degrees, lat_total), lambda g, low: (g, 0, 0)),
+                pl.BlockSpec((PAIR_STEP, lat_total, degrees), lambda g, low: (g, 0, 0)),
                 pl.BlockSpec((channels, channels), lambda g, low: (0, 0)),
             ],
             out_specs=[
@@ -320,7 +317,7 @@
     coeffs, out_ref, scratch = rest[:-2], rest[-2], rest[-1]
     step = pl.program_id(0)
     _, degrees, channels = out_ref.shape
-    lat_total = legendre_ref.shape[2]
+    lat_total = legendre_ref.shape[1]
     rows = 2 * PAIR_STEP
     devices = coeffs[0].shape[0]
     per_device = lat_total // devices
@@ -351,15 +348,18 @@
                     preferred_element_type=jnp.float32,
                 ).astype(jnp.bfloat16)
             )
-        both = jnp.dot(
-            legendre_ref[i], jnp.concatenate(sides, axis=1), preferred_element_type=jnp.float32
+        both = lax.dot_general(
+            legendre_ref[i],
+            jnp.concatenate(sides, axis=1),
+            (((0,), (0,)), ((), ())),
+            preferred_element_type=jnp.float32,
         )
         lower = degree < degrees - 1 - low
         out_ref[i] = jnp.where(lower, both[:, :channels], both[:, channels:]).astype(jnp.bfloat16)
 
 
 def forward_legendre(coeffs, legendre, local_low, order, spans):
-    pair_count, degrees, lat_total = legendre.shape
+    pair_count, lat_total, degrees = legendre.shape
     channels = order.shape[0]
     rows = 2 * PAIR_STEP
     devices = coeffs[0].shape[0]
@@ -369,7 +369,7 @@
             num_scalar_prefetch=1,
             grid=(pair_count // PAIR_STEP,),
             in_specs=[
-                pl.BlockSpec((PAIR_STEP, degrees, lat_total), lambda g, low: (g, 0, 0)),
+                pl.BlockSpec((PAIR_STEP, lat_total, degrees), lambda g, low: (g, 0, 0)),
                 pl.BlockSpec((channels, channels), lambda g, low: (0, 0)),
             ]
             + [
@@ -448,9 +448,9 @@
 
 def row_spans(lat_rows):
     pairs = lat_rows // 2
-    parts = math.gcd(pairs, ROW_PARTS)
-    count = pairs // parts * 2
-    return [(part * count, count) for part in range(parts)]
+    first = max(1, pairs * 7 // 10)
+    spans = [(0, 2 * first), (2 * first, 2 * (pairs - first))]
+    return [span for span in spans if span[1] > 0]
 
 
 def on_device_kernels(spectral, legendre, pair_low, routes, w_in, w_mid, w_out):
@@ -463,7 +463,10 @@
     spans = row_spans(lat_rows)
     local_low = lax.dynamic_slice_in_dim(pair_low, lax.axis_index("wave") * pair_count, pair_count)
     order = channel_order(channels)
-    sent = inverse_legendre(spectral, legendre, local_low, order, spans, devices)
+    turned = jnp.swapaxes(legendre, 1, 2)
+    sent = inverse_legendre(spectral, turned, local_low, order, spans, devices)
+    pair_low, routes, *sent = lax.optimization_barrier((pair_low, routes, *sent))
+    arriving = exchange(sent[0])
     inverse_table, forward_table = phase_tables(slot_waves(pair_low, wave_total), NLON)
     regimes = routes[:, 0]
     total_columns = regimes.shape[0]
@@ -474,8 +477,16 @@
     outgoing = jnp.zeros((SLOT_PARTS * devices * slots, feat), jnp.bfloat16)
     forced = []
     width = NLON // 4
-    for part, (first, count) in zip(sent, spans):
-        forced_part, columns = to_grid(exchange(part), inverse_table)
+    for part, (first, count) in enumerate(spans):
+        held = (arriving, sent[part + 1 :], inverse_table, forward_table, places, outgoing)
+        arriving, later, inverse_table, forward_table, places, outgoing = lax.optimization_barrier(
+            held
+        )
+        arrived = arriving
+        if later:
+            sent[part + 1 :] = later
+            arriving = exchange(sent[part + 1])
+        forced_part, columns = to_grid(arrived, inverse_table)
         forced.append(forced_part)
         at = places[first // 2 * width : (first + count) // 2 * width]
         outgoing = outgoing.at[at].set(columns, unique_indices=True, mode="promise_in_bounds")
@@ -485,12 +496,13 @@
         for part in range(SLOT_PARTS)
     ]
     incoming = jnp.concatenate(answers, axis=0).reshape(-1, feat)
-    received = []
-    for forced_part, (first, count) in zip(forced, spans):
+    received = [None] * len(spans)
+    for part in reversed(range(len(spans))):
+        first, count = spans[part]
         at = places[first // 2 * width : (first + count) // 2 * width]
         returned = incoming.at[at].get(mode="promise_in_bounds")
-        received.append(exchange(to_fourier(forced_part, returned, forward_table, devices)))
-    return forward_legendre(received, legendre, local_low, order, spans)
+        received[part] = exchange(to_fourier(forced[part], returned, forward_table, devices))
+    return forward_legendre(received, turned, local_low, order, spans)
 
 
 def on_device(spectral, legendre, pair_low, routes, w_in, w_mid, w_out):

time: 566 us -> 474 us (0.84); the launches traced: 556 us -> 473 us
  blocking collectives: 177 us -> 143 us
  local copies, waits for them, and re-layouts: 56.9 us -> 30.1 us
  Pallas kernels: 116 us -> 101 us
  starting transfers between devices: 54.2 us -> 48.4 us
    all_to_all x5 -> x2, blocking collectives: 177 us -> 143 us  [exchange(): lax.all_to_all(values, 'wave', split_axis=0, concat_axis=0, tiled=True)]
    unnamed x17 -> x6, local copies, waits for them, and re-layouts: 14 us -> 0.01 us
    scatter x5 -> x2, local copies, waits for them, and re-layouts: 27.7 us -> 16.7 us  [on_device_kernels(): outgoing.at[at].set(columns, unique_indices=True, mode='promise_in_bounds')]
    pallas_call x5 -> x2, Pallas kernels: 27.5 us -> 19.6 us  [to_grid(): pl.pallas_call(grid_kernel, grid=(lats // 2,), in_specs=[pl.BlockSpec((de...]
    pallas_call x5 -> x2, Pallas kernels: 27.4 us -> 20.2 us  [to_fourier(): pl.pallas_call(fourier_kernel, grid=(lats // 2,), in_specs=[pl.BlockSpec(...]
    all_to_all x9 -> x6, starting transfers between devices: 54.2 us -> 48.4 us  [exchange(): lax.all_to_all(values, 'wave', split_axis=0, concat_axis=0, tiled=True)]
    all_to_all x9 -> x6, waiting for transfers between devices: 113 us -> 110 us  [exchange(): lax.all_to_all(values, 'wave', split_axis=0, concat_axis=0, tiled=True)]
    gather x5 -> x2, local copies, waits for them, and re-layouts: 12.6 us -> 9.9 us  [on_device_kernels(): returned = incoming.at[at].get(mode='promise_in_bounds')]
  transfers between devices with their start and end apart: 9 -> 6, of which waited for: 8 -> 6; matrix products, arithmetic and copies ran while one was open for 13% -> 12% of each run, Pallas kernels for 13% -> 11%
where the time goes in v2:
time: 474 us; the launch traced here: 473 us
  blocking collectives  143 us (30%)
  waiting for transfers between devices  110 us (23%)
  Pallas kernels  101 us (21%)
  starting transfers between devices  48.4 us (10%)
  other arithmetic  40.6 us (9%)
  local copies, waits for them, and re-layouts  30.1 us (6%)
    all_to_all x2, blocking collectives, exchange(): lax.all_to_all(values, 'wave', split_axis=0, concat_axis=0, tiled=True)  143 us
    all_to_all x6, waiting for transfers between devices, exchange(): lax.all_to_all(values, 'wave', split_axis=0, concat_axis=0, tiled=True)  110 us
    all_to_all x6, starting transfers between devices, exchange(): lax.all_to_all(values, 'wave', split_axis=0, concat_axis=0, tiled=True)  48.4 us
    another operation x5, other arithmetic  33.8 us
    pallas_call x2, Pallas kernels, run_network(): pl.pallas_call(network_kernel, grid=(devices // group,), in_specs=[pl.Blo...  28.6 us
    pallas_call x2, Pallas kernels, to_fourier(): pl.pallas_call(fourier_kernel, grid=(lats // 2,), in_specs=[pl.BlockSpec(...  20.2 us
    pallas_call x2, Pallas kernels, to_grid(): pl.pallas_call(grid_kernel, grid=(lats // 2,), in_specs=[pl.BlockSpec((de...  19.6 us
    pallas_call x1, Pallas kernels, forward_legendre(): pl.pallas_call(functools.partial(forward_kernel, spans), grid_spec=pltpu....  16.7 us
  transfers between devices with their start and end apart: 6, of which 6 were waited for; matrix products, arithmetic and copies ran while one was open for 12% of the time, Pallas kernels for 11%

profile of v2, /device:TPU:1, one launch (start us, length us, event | category | flops | bytes accessed | tf_op | source)
XLA Modules:
  0.0 472.5 jit_solution(13554643849474349852)
XLA Ops:
  0.0 0.8 fusion.10.order_ref
  0.8 1.3 dynamic_slice.3.low_ref
  2.1 15.4 %inverse_legendre.1 = (bf16[16,14,40,256]{3,2,1,0:T(8,128)(2,1)}, bf16[16,6,40,256]{3,2,1,0:T(8,128)(2,1)}) custom-call(s32[20]{0:T(128)} %dynamic_slice.3.low_ref, bf16[20,641,256]{2,1,0:T(8,128)(2,1)} %spectral_ref.1, bf16[20,320,641]{2,1,0:T(8,128)(2,1)} %bitcast.15, bf16[256,256]{1,0:T(8,128)(2,1)} %fusion.10.order_ref), custom_call_target="tpu_custom_call" | custom-call | flops 4200857600 | bytes 21332480 | tf_op jit(solution)/shard_map/inverse_legendre/pallas_call | solution.py:190
  17.4 0.0 copy-start.2
  17.4 0.0 copy-start.1
  17.5 7.5 %all-to-all-start = ((bf16[16,14,40,256]{3,2,1,0:T(8,128)(2,1)}), bf16[16,14,40,256]{3,2,1,0:T(8,128)(2,1)}, u32[]{:S(2)}, u32[]{:S(2)}) async-start(bf16[16,14,40,256]{3,2,1,0:T(8,128)(2,1)} %get-tuple-element.28), calls=%async_computation | async-start | bytes 9175040 | tf_op jit(solution)/shard_map/all_to_all | solution.py:446
  24.9 0.0 copy-done.2
  25.0 0.1 copy.8
  25.1 0.1 reshape.163
  25.3 0.0 copy-done.1
  25.4 4.6 reduce-window.6
  30.1 0.5 slice_reduce_fusion
  30.5 0.2 reduce-window.9
  30.7 0.1 broadcast.152
  30.9 0.1 fusion.11
  31.0 15.0 %multiply_convert_fusion.1 = (bf16[640,1280]{1,0:T(8,128)(2,1)S(1)}, bf16[640,1280]{1,0:T(8,128)(2,1)S(1)}) fusion(s32[640]{0:T(1024)S(1)} %reshape.163), kind=kLoop, calls=%fused_computation.13 | loop fusion | flops 10649600 | bytes 3279360 | tf_op jit(solution)/shard_map/convert.2
  46.1 13.9 %multiply_convert_fusion.3 = (bf16[1280,640]{1,0:T(8,128)(2,1)S(1)}, bf16[1280,640]{1,0:T(8,128)(2,1)S(1)}) fusion(s32[640]{0:T(1024)S(1)} %reshape.163, f32[640]{0:T(1024)S(1)} %get-tuple-element.53, f32[640]{0:T(1024)S(1)} %get-tuple-element.54), kind=kLoop, calls=%fused_computation.18 | loop fusion | flops 10649600 | bytes 3284480 | tf_op jit(solution)/shard_map/convert.4
  60.0 5.7 %pad_maximum_fusion = (bf16[1280,1280]{1,0:T(8,128)(2,1)}, bf16[1280,1280]{1,0:T(8,128)(2,1)}) fusion(bf16[1280,640]{1,0:T(8,128)(2,1)S(1)} %get-tuple-element.52, bf16[1280,640]{1,0:T(8,128)(2,1)S(1)} %get-tuple-element.51, bf16[640,1280]{1,0:T(8,128)(2,1)S(1)} %get-tuple-element.50, bf16[640,1280]{1,0:T(8,128)(2,1)S(1)} %get-tuple-element.49), kind=kLoop, calls=%fused_computation.10 | loop fusion | flops 13107200 | bytes 13107200 | tf_op jit(solution)/shard_map/concatenate | solution.py:439
  65.6 44.3 %all-to-all-done.coeff_ref = bf16[16,14,40,256]{3,2,1,0:T(8,128)(2,1)} async-done(((bf16[16,14,40,256]{3,2,1,0:T(8,128)(2,1)}), bf16[16,14,40,256]{3,2,1,0:T(8,128)(2,1)}, u32[]{:S(2)}, u32[]{:S(2)}) %all-to-all-start) | async-done | bytes 4587552 | tf_op jit(solution)/shard_map/all_to_all | solution.py:446
  109.9 20.7 %all-to-all-start.1 = ((bf16[16,6,40,256]{3,2,1,0:T(8,128)(2,1)}), bf16[16,6,40,256]{3,2,1,0:T(8,128)(2,1)}, u32[]{:S(2)}, u32[]{:S(2)}) async-start(bf16[16,6,40,256]{3,2,1,0:T(8,128)(2,1)} %get-tuple-element.35), calls=%async_computation.1 | async-start | bytes 3932160 | tf_op jit(solution)/shard_map/all_to_all | solution.py:446
  130.6 12.6 %to_grid.2 = (f32[14,1280,128]{2,1,0:T(8,128)}, bf16[2240,128]{1,0:T(8,128)(2,1)}) custom-call(bf16[16,14,40,256]{3,2,1,0:T(8,128)(2,1)} %all-to-all-done.coeff_ref, bf16[1280,1280]{1,0:T(8,128)(2,1)} %get-tuple-element.43.table_ref), custom_call_target="tpu_custom_call" | custom-call | flops 5872025600 | bytes 7864320 | tf_op jit(solution)/shard_map/to_grid/pallas_call | solution.py:247
  143.2 0.2 broadcast_in_dim.29
  143.4 11.1 %scatter_fusion = bf16[6400,128]{1,0:T(8,128)(2,1)S(1)} fusion(bf16[6400,128]{1,0:T(8,128)(2,1)S(1)} %broadcast_in_dim.29, s32[2240]{0:T(1024)S(1)} %compare_select_fusion.1, bf16[2240,128]{1,0:T(8,128)(2,1)} %get-tuple-element.39), kind=kCustom, calls=%fused_computation.2 | custom fusion | bytes 1729280 | tf_op jit(solution)/shard_map/scatter | solution.py:492
  154.6 15.4 %all-to-all-done.1.coeff_ref = bf16[16,6,40,256]{3,2,1,0:T(8,128)(2,1)} async-done(((bf16[16,6,40,256]{3,2,1,0:T(8,128)(2,1)}), bf16[16,6,40,256]{3,2,1,0:T(8,128)(2,1)}, u32[]{:S(2)}, u32[]{:S(2)}) %all-to-all-start.1) | async-done | bytes 1966112 | tf_op jit(solution)/shard_map/all_to_all | solution.py:446
  170.0 0.1 compare_select_fusion.2
  170.0 7.0 %to_grid.3 = (f32[6,1280,128]{2,1,0:T(8,128)}, bf16[960,128]{1,0:T(8,128)(2,1)}) custom-call(bf16[16,6,40,256]{3,2,1,0:T(8,128)(2,1)} %all-to-all-done.1.coeff_ref, bf16[1280,1280]{1,0:T(8,128)(2,1)} %get-tuple-element.43.table_ref), custom_call_target="tpu_custom_call" | custom-call | flops 2516582400 | bytes 5242880 | tf_op jit(solution)/shard_map/to_grid/pallas_call | solution.py:247
  177.1 5.5 %scatter_fusion.1 = bf16[6400,128]{1,0:T(8,128)(2,1)S(1)} fusion(bf16[6400,128]{1,0:T(8,128)(2,1)S(1)} %scatter_fusion, s32[960]{0:T(1024)S(1)} %compare_select_fusion.2, bf16[960,128]{1,0:T(8,128)(2,1)} %get-tuple-element.44), kind=kCustom, calls=%fused_computation.3 | custom fusion | bytes 741120 | tf_op jit(solution)/shard_map/scatter | solution.py:492
  182.6 1.0 fusion.22
  183.6 31.3 %all_to_all.40.rows_ref = bf16[16,200,128]{2,1,0:T(8,128)(2,1)} all-to-all(bf16[16,200,128]{2,1,0:T(8,128)(2,1)S(1)} %bitcast.17), channel_id=1, replica_groups=mesh['grp'=2,'wave'=16] {'wave'}, dimensions={0} | all-to-all | bytes 1638400 | tf_op jit(solution)/shard_map/all_to_all | solution.py:446
  214.9 3.5 all-to-all-start.4
  218.4 14.3 %network.2 = bf16[16,200,128]{2,1,0:T(8,128)(2,1)} custom-call(bf16[16,200,128]{2,1,0:T(8,128)(2,1)} %all_to_all.40.rows_ref, bf16[1,128,1024]{2,1,0:T(8,128)(2,1)} %in_ref.3, bf16[1,1024,1024]{2,1,0:T(8,128)(2,1)} %mid_ref.3, bf16[1,1024,128]{2,1,0:T(8,128)(2,1)} %out_w_ref.3), custom_call_target="tpu_custom_call" | custom-call | flops 8388608000 | bytes 3735552 | tf_op jit(solution)/shard_map/network/pallas_call | solution.py:411
  232.7 4.9 %all-to-all-done.4.rows_ref = bf16[16,200,128]{2,1,0:T(8,128)(2,1)S(1)} async-done(((bf16[16,200,128]{2,1,0:T(8,128)(2,1)}), bf16[16,200,128]{2,1,0:T(8,128)(2,1)S(1)}, u32[]{:S(2)}, u32[]{:S(2)}) %all-to-all-start.4) | async-done | bytes 819232 | tf_op jit(solution)/shard_map/all_to_all | solution.py:446
  237.6 0.0 copy-start
  237.6 5.6 %all-to-all-start.3 = ((bf16[16,200,128]{2,1,0:T(8,128)(2,1)}), bf16[16,200,128]{2,1,0:T(8,128)(2,1)S(1)}, u32[]{:S(2)}, u32[]{:S(2)}) async-start(bf16[16,200,128]{2,1,0:T(8,128)(2,1)} %network.2), calls=%async_computation.3 | async-start | bytes 1638400 | tf_op jit(solution)/shard_map/all_to_all | solution.py:446
  243.2 0.0 copy-done
  243.2 14.3 %network.3 = bf16[16,200,128]{2,1,0:T(8,128)(2,1)} custom-call(bf16[16,200,128]{2,1,0:T(8,128)(2,1)} %copy-done, bf16[1,128,1024]{2,1,0:T(8,128)(2,1)} %in_ref.3, bf16[1,1024,1024]{2,1,0:T(8,128)(2,1)} %mid_ref.3, bf16[1,1024,128]{2,1,0:T(8,128)(2,1)} %out_w_ref.3), custom_call_target="tpu_custom_call" | custom-call | flops 8388608000 | bytes 3735552 | tf_op jit(solution)/shard_map/network/pallas_call | solution.py:411
  257.5 4.9 %all-to-all-done.3 = bf16[16,200,128]{2,1,0:T(8,128)(2,1)S(1)} async-done(((bf16[16,200,128]{2,1,0:T(8,128)(2,1)}), bf16[16,200,128]{2,1,0:T(8,128)(2,1)S(1)}, u32[]{:S(2)}, u32[]{:S(2)}) %all-to-all-start.3) | async-done | bytes 819232 | tf_op jit(solution)/shard_map/all_to_all | solution.py:446
  262.4 5.6 %all-to-all-start.5 = ((bf16[16,200,128]{2,1,0:T(8,128)(2,1)}), bf16[16,200,128]{2,1,0:T(8,128)(2,1)S(1)}, u32[]{:S(2)}, u32[]{:S(2)}) async-start(bf16[16,200,128]{2,1,0:T(8,128)(2,1)} %network.3), calls=%async_computation.5 | async-start | bytes 1638400 | tf_op jit(solution)/shard_map/all_to_all | solution.py:446
  267.9 19.2 %all-to-all-done.5 = bf16[16,200,128]{2,1,0:T(8,128)(2,1)S(1)} async-done(((bf16[16,200,128]{2,1,0:T(8,128)(2,1)}), bf16[16,200,128]{2,1,0:T(8,128)(2,1)S(1)}, u32[]{:S(2)}, u32[]{:S(2)}) %all-to-all-start.5) | async-done | bytes 819232 | tf_op jit(solution)/shard_map/all_to_all | solution.py:446
  287.1 0.1 pad_maximum_fusion.2
  287.3 4.3 gather_fusion.1
  291.6 7.5 %to_fourier.3 = bf16[16,6,40,256]{3,2,1,0:T(8,128)(2,1)} custom-call(f32[6,1280,128]{2,1,0:T(8,128)} %get-tuple-element.46.forced_ref, bf16[960,128]{1,0:T(8,128)(2,1)} %gather_fusion.1, bf16[1280,1280]{1,0:T(8,128)(2,1)} %get-tuple-element.45.table_ref), custom_call_target="tpu_custom_call" | custom-call | flops 2516582400 | bytes 7208960 | tf_op jit(solution)/shard_map/to_fourier/pallas_call | solution.py:300
  299.0 5.6 %all-to-all-start.7 = ((bf16[16,6,40,256]{3,2,1,0:T(8,128)(2,1)}), bf16[16,6,40,256]{3,2,1,0:T(8,128)(2,1)}, u32[]{:S(2)}, u32[]{:S(2)}) async-start(bf16[16,6,40,256]{3,2,1,0:T(8,128)(2,1)} %to_fourier.3), calls=%async_computation.7 | async-start | bytes 3932160 | tf_op jit(solution)/shard_map/all_to_all | solution.py:446
  304.6 5.6 %gather_fusion = bf16[2240,128]{1,0:T(8,128)(2,1)} fusion(bf16[6400,128]{1,0:T(8,128)(2,1)S(1)} %bitcast.14, s32[3072]{0:T(1024)S(1)} %pad_clamp_fusion), kind=kCustom, calls=%fused_computation | custom fusion | bytes 1155840 | tf_op jit(solution)/shard_map/gather | solution.py:503
  310.2 12.8 %to_fourier.2 = bf16[16,14,40,256]{3,2,1,0:T(8,128)(2,1)} custom-call(f32[14,1280,128]{2,1,0:T(8,128)} %get-tuple-element.34.forced_ref, bf16[2240,128]{1,0:T(8,128)(2,1)} %gather_fusion, bf16[1280,1280]{1,0:T(8,128)(2,1)} %get-tuple-element.45.table_ref), custom_call_target="tpu_custom_call" | custom-call | flops 5872025600 | bytes 12451840 | tf_op jit(solution)/shard_map/to_fourier/pallas_call | solution.py:300
  323.0 20.9 %all-to-all-done.7.rest_1_ = bf16[16,6,40,256]{3,2,1,0:T(8,128)(2,1)} async-done(((bf16[16,6,40,256]{3,2,1,0:T(8,128)(2,1)}), bf16[16,6,40,256]{3,2,1,0:T(8,128)(2,1)}, u32[]{:S(2)}, u32[]{:S(2)}) %all-to-all-start.7) | async-done | bytes 1966112 | tf_op jit(solution)/shard_map/all_to_all | solution.py:446
  344.0 111.8 %all_to_all.41.rest_0_ = bf16[16,14,40,256]{3,2,1,0:T(8,128)(2,1)} all-to-all(bf16[16,14,40,256]{3,2,1,0:T(8,128)(2,1)} %to_fourier.2), channel_id=1, replica_groups=mesh['grp'=2,'wave'=16] {'wave'}, dimensions={0} | all-to-all | bytes 9175040 | tf_op jit(solution)/shard_map/all_to_all | solution.py:446
  455.8 16.7 %forward_legendre.1 = bf16[20,641,256]{2,1,0:T(8,128)(2,1)} custom-call(s32[20]{0:T(128)} %dynamic_slice.3.low_ref, bf16[20,320,641]{2,1,0:T(8,128)(2,1)} %bitcast.16, bf16[256,256]{1,0:T(8,128)(2,1)} %fusion.10.order_ref, bf16[16,14,40,256]{3,2,1,0:T(8,128)(2,1)} %all_to_all.41.rest_0_, bf16[16,6,40,256]{3,2,1,0:T(8,128)(2,1)} %all-to-all-done.7.rest_1_), custom_call_target="tpu_custom_call" | custom-call | flops 4200857600 | bytes 16409600 | tf_op jit(solution)/shard_map/forward_legendre/pallas_call | solution.py:366
  (17 shorter events, 0.3 us)
Async XLA Ops:
  17.4 7.5 %copy-start.2 = (s32[320]{0:T(512)S(1)}, s32[320]{0:T(512)}, u32[]{:S(2)}) copy-start(s32[320]{0:T(512)} %param.9) | copy-start | bytes 3844
  17.4 7.8 %copy-start.1 = (s32[3200,1]{0,1:T(1,128)S(1)}, s32[3200,1]{0,1:T(1,128)}, u32[]{:S(2)}) copy-start(s32[3200,1]{0,1:T(1,128)} %param.10) | copy-start | bytes 38404
  17.5 92.5 %all-to-all-start = ((bf16[16,14,40,256]{3,2,1,0:T(8,128)(2,1)}), bf16[16,14,40,256]{3,2,1,0:T(8,128)(2,1)}, u32[]{:S(2)}, u32[]{:S(2)}) async-start(bf16[16,14,40,256]{3,2,1,0:T(8,128)(2,1)} %get-tuple-element.28), calls=%async_computation | async-start | bytes 9175040 | tf_op jit(solution)/shard_map/all_to_all | solution.py:446
  109.9 60.0 %all-to-all-start.1 = ((bf16[16,6,40,256]{3,2,1,0:T(8,128)(2,1)}), bf16[16,6,40,256]{3,2,1,0:T(8,128)(2,1)}, u32[]{:S(2)}, u32[]{:S(2)}) async-start(bf16[16,6,40,256]{3,2,1,0:T(8,128)(2,1)} %get-tuple-element.35), calls=%async_computation.1 | async-start | bytes 3932160 | tf_op jit(solution)/shard_map/all_to_all | solution.py:446
  214.9 22.7 %all-to-all-start.4 = ((bf16[16,200,128]{2,1,0:T(8,128)(2,1)}), bf16[16,200,128]{2,1,0:T(8,128)(2,1)S(1)}, u32[]{:S(2)}, u32[]{:S(2)}) async-start(bf16[16,200,128]{2,1,0:T(8,128)(2,1)} %bitcast.5), calls=%async_computation.4 | async-start | bytes 1638400 | tf_op jit(solution)/shard_map/all_to_all | solution.py:446
  237.6 5.6 %copy-start = (bf16[16,200,128]{2,1,0:T(8,128)(2,1)}, bf16[16,200,128]{2,1,0:T(8,128)(2,1)S(1)}, u32[]{:S(2)}) copy-start(bf16[16,200,128]{2,1,0:T(8,128)(2,1)S(1)} %all-to-all-done.4.rows_ref) | copy-start | bytes 2457604
  237.6 24.8 %all-to-all-start.3 = ((bf16[16,200,128]{2,1,0:T(8,128)(2,1)}), bf16[16,200,128]{2,1,0:T(8,128)(2,1)S(1)}, u32[]{:S(2)}, u32[]{:S(2)}) async-start(bf16[16,200,128]{2,1,0:T(8,128)(2,1)} %network.2), calls=%async_computation.3 | async-start | bytes 1638400 | tf_op jit(solution)/shard_map/all_to_all | solution.py:446
  262.4 24.8 %all-to-all-start.5 = ((bf16[16,200,128]{2,1,0:T(8,128)(2,1)}), bf16[16,200,128]{2,1,0:T(8,128)(2,1)S(1)}, u32[]{:S(2)}, u32[]{:S(2)}) async-start(bf16[16,200,128]{2,1,0:T(8,128)(2,1)} %network.3), calls=%async_computation.5 | async-start | bytes 1638400 | tf_op jit(solution)/shard_map/all_to_all | solution.py:446
  299.0 44.9 %all-to-all-start.7 = ((bf16[16,6,40,256]{3,2,1,0:T(8,128)(2,1)}), bf16[16,6,40,256]{3,2,1,0:T(8,128)(2,1)}, u32[]{:S(2)}, u32[]{:S(2)}) async-start(bf16[16,6,40,256]{3,2,1,0:T(8,128)(2,1)} %to_fourier.3), calls=%async_computation.7 | async-start | bytes 3932160 | tf_op jit(solution)/shard_map/all_to_all | solution.py:446

commit v3 on v2

--- a/solution.py
+++ b/solution.py
@@ -11,7 +11,6 @@
 NLON = 1280
 FIELDS = 4
 PAIR_STEP = 4
-SLOT_PARTS = 2
 
 
 def slot_waves(pair_low, wave_total):
@@ -392,38 +391,92 @@
     return half + half * jnp.tanh(half)
 
 
-def network_kernel(rows_ref, in_ref, mid_ref, out_w_ref, out_ref):
-    sources, slots, feat = rows_ref.shape
-    rows = rows_ref[...].reshape(sources * slots, feat)
-    hidden = smooth(jnp.dot(rows, in_ref[0], preferred_element_type=jnp.float32))
-    deeper = smooth(
-        jnp.dot(hidden.astype(jnp.bfloat16), mid_ref[0], preferred_element_type=jnp.float32)
-    )
-    answer = jnp.dot(
-        deeper.astype(jnp.bfloat16), out_w_ref[0], preferred_element_type=jnp.float32
-    )
-    out_ref[...] = answer.reshape(sources, slots, feat).astype(jnp.bfloat16)
-
-
-def run_network(arrived, w_in, w_mid, w_out):
-    devices, slots, feat = arrived.shape
-    group = math.gcd(devices, 4)
+def network_kernel(
+    sent_ref, in_ref, mid_ref, out_ref, result_ref, arrived, answers, sends, arrivals, backs, returns
+):
+    devices = sent_ref.shape[0]
+    me = lax.axis_index("wave")
+    barrier = pltpu.get_barrier_semaphore()
+
+    def peer(k):
+        return lax.rem(me + k, devices)
+
+    def outward(k, source, target):
+        return pltpu.make_async_remote_copy(
+            src_ref=sent_ref.at[target],
+            dst_ref=arrived.at[source],
+            send_sem=sends.at[k],
+            recv_sem=arrivals.at[k],
+            device_id={"wave": peer(k)},
+            device_id_type=pl.DeviceIdType.MESH,
+        )
+
+    def backward(k, source, owner):
+        return pltpu.make_async_remote_copy(
+            src_ref=answers.at[source],
+            dst_ref=result_ref.at[owner],
+            send_sem=backs.at[k],
+            recv_sem=returns.at[k],
+            device_id={"wave": peer(devices - k)},
+            device_id_type=pl.DeviceIdType.MESH,
+        )
+
+    def answer(rows):
+        hidden = smooth(jnp.dot(rows, in_ref[0], preferred_element_type=jnp.float32))
+        deeper = smooth(
+            jnp.dot(hidden.astype(jnp.bfloat16), mid_ref[0], preferred_element_type=jnp.float32)
+        )
+        return jnp.dot(
+            deeper.astype(jnp.bfloat16), out_ref[0], preferred_element_type=jnp.float32
+        ).astype(jnp.bfloat16)
+
+    def greet(k, carry):
+        pl.semaphore_signal(
+            barrier, inc=1, device_id={"wave": peer(k)}, device_id_type=pl.DeviceIdType.MESH
+        )
+        return carry
+
+    def send(k, carry):
+        outward(k, me, peer(k)).start()
+        return carry
+
+    def serve(k, carry):
+        source = peer(devices - k)
+        outward(k, source, peer(k)).wait_recv()
+        answers[source] = answer(arrived[source])
+        backward(k, source, me).start()
+        return carry
+
+    def finish(k, carry):
+        outward(k, me, peer(k)).wait_send()
+        backward(k, peer(devices - k), me).wait_send()
+        backward(k, peer(k), peer(k)).wait_recv()
+        return carry
+
+    lax.fori_loop(1, devices, greet, 0)
+    pl.semaphore_wait(barrier, devices - 1)
+    lax.fori_loop(1, devices, send, 0)
+    result_ref[me] = answer(sent_ref[me])
+    lax.fori_loop(1, devices, serve, 0)
+    lax.fori_loop(1, devices, finish, 0)
+
+
+def run_network(outgoing, w_in, w_mid, w_out):
+    devices, slots, feat = outgoing.shape
     return pl.pallas_call(
         network_kernel,
-        grid=(devices // group,),
-        in_specs=[
-            pl.BlockSpec((group, slots, feat), lambda i: (i, 0, 0)),
-            pl.BlockSpec(w_in.shape, lambda i: (0, 0, 0)),
-            pl.BlockSpec(w_mid.shape, lambda i: (0, 0, 0)),
-            pl.BlockSpec(w_out.shape, lambda i: (0, 0, 0)),
-        ],
-        out_specs=pl.BlockSpec((group, slots, feat), lambda i: (i, 0, 0)),
-        out_shape=jax.ShapeDtypeStruct(arrived.shape, jnp.bfloat16),
+        in_specs=[pl.BlockSpec(memory_space=pltpu.VMEM)] * 4,
+        out_specs=pl.BlockSpec(memory_space=pltpu.VMEM),
+        out_shape=jax.ShapeDtypeStruct(outgoing.shape, jnp.bfloat16),
+        scratch_shapes=[pltpu.VMEM(outgoing.shape, jnp.bfloat16)] * 2
+        + [pltpu.SemaphoreType.DMA((devices,))] * 4,
+        compiler_params=pltpu.CompilerParams(collective_id=0, has_side_effects=True),
         name="network",
         cost_estimate=cost(
-            2 * devices * slots * (w_in.size + w_mid.size + w_out.size), 4 * arrived.size + 2 * w_mid.size
+            2 * devices * slots * (w_in.size + w_mid.size + w_out.size),
+            4 * outgoing.size + 2 * w_mid.size,
         ),
-    )(arrived, w_in, w_mid, w_out)
+    )(outgoing, w_in, w_mid, w_out)
 
 
 def phase_tables(wavenums, points):
@@ -448,7 +501,7 @@
 
 def row_spans(lat_rows):
     pairs = lat_rows // 2
-    first = max(1, pairs * 7 // 10)
+    first = max(1, pairs * 4 // 5)
     spans = [(0, 2 * first), (2 * first, 2 * (pairs - first))]
     return [span for span in spans if span[1] > 0]
 
@@ -472,9 +525,8 @@
     total_columns = regimes.shape[0]
     positions = slot_positions(regimes.reshape(1, -1), devices)[0]
     capacity = 2 * total_columns // devices
-    slots = capacity // SLOT_PARTS
-    places = (positions // slots * devices + regimes) * slots + positions % slots
-    outgoing = jnp.zeros((SLOT_PARTS * devices * slots, feat), jnp.bfloat16)
+    places = regimes * capacity + positions
+    outgoing = jnp.zeros((devices * capacity, feat), jnp.bfloat16)
     forced = []
     width = NLON // 4
     for part, (first, count) in enumerate(spans):
@@ -490,12 +542,8 @@
         forced.append(forced_part)
         at = places[first // 2 * width : (first + count) // 2 * width]
         outgoing = outgoing.at[at].set(columns, unique_indices=True, mode="promise_in_bounds")
-    outgoing = outgoing.reshape(SLOT_PARTS, devices, slots, feat)
-    answers = [
-        exchange(run_network(exchange(outgoing[part]), w_in, w_mid, w_out))
-        for part in range(SLOT_PARTS)
-    ]
-    incoming = jnp.concatenate(answers, axis=0).reshape(-1, feat)
+    incoming = run_network(outgoing.reshape(devices, capacity, feat), w_in, w_mid, w_out)
+    incoming = incoming.reshape(-1, feat)
     received = [None] * len(spans)
     for part in reversed(range(len(spans))):
         first, count = spans[part]
@@ -511,7 +559,7 @@
         spectral.shape[0] % PAIR_STEP == 0
         and 2 * spectral.shape[0] % 8 == 0
         and legendre.shape[2] // devices % 2 == 0
-        and 2 * routes.shape[0] // devices % (8 * SLOT_PARTS) == 0
+        and 2 * routes.shape[0] // devices % 8 == 0
     )
     body = on_device_kernels if aligned else on_device_arrays
     return body(spectral, legendre, pair_low, routes, w_in, w_mid, w_out)

time: 474 us -> 453 us (0.956)
  Pallas kernels: 101 us -> 155 us
  waiting for transfers between devices: 110 us -> 68.7 us
  blocking collectives: 143 us -> 123 us
  starting transfers between devices: 48.4 us -> 36.1 us
    pallas_call x2 -> x1, Pallas kernels: 28.6 us -> 83.7 us  [run_network(): pl.pallas_call(network_kernel, in_specs=[pl.BlockSpec(memory_space=pltpu....]
    all_to_all x6 -> x3, waiting for transfers between devices: 110 us -> 68.7 us  [exchange(): lax.all_to_all(values, 'wave', split_axis=0, concat_axis=0, tiled=True)]
    all_to_all x2 -> x1, blocking collectives: 143 us -> 123 us  [exchange(): lax.all_to_all(values, 'wave', split_axis=0, concat_axis=0, tiled=True)]
    all_to_all x6 -> x3, starting transfers between devices: 48.4 us -> 36.1 us  [exchange(): lax.all_to_all(values, 'wave', split_axis=0, concat_axis=0, tiled=True)]
  transfers between devices with their start and end apart: 6 -> 3, of which waited for: 6 -> 3; matrix products, arithmetic and copies ran while one was open for 12% -> 12% of each run, Pallas kernels for 11% -> 6%
where the time goes in v3:
time: 453 us; the launch traced here: 452 us
  Pallas kernels  155 us (34%)
  blocking collectives  123 us (27%)
  waiting for transfers between devices  68.7 us (15%)
  other arithmetic  40.4 us (9%)
  starting transfers between devices  36.1 us (8%)
  local copies, waits for them, and re-layouts  28.8 us (6%)
    all_to_all x1, blocking collectives, exchange(): lax.all_to_all(values, 'wave', split_axis=0, concat_axis=0, tiled=True)  123 us
    pallas_call x1, Pallas kernels, run_network(): pl.pallas_call(network_kernel, in_specs=[pl.BlockSpec(memory_space=pltpu....  83.7 us
    all_to_all x3, waiting for transfers between devices, exchange(): lax.all_to_all(values, 'wave', split_axis=0, concat_axis=0, tiled=True)  68.7 us
    all_to_all x3, starting transfers between devices, exchange(): lax.all_to_all(values, 'wave', split_axis=0, concat_axis=0, tiled=True)  36.1 us
    another operation x5, other arithmetic  33.8 us
    pallas_call x2, Pallas kernels, to_fourier(): pl.pallas_call(fourier_kernel, grid=(lats // 2,), in_specs=[pl.BlockSpec(...  19.7 us
    pallas_call x2, Pallas kernels, to_grid(): pl.pallas_call(grid_kernel, grid=(lats // 2,), in_specs=[pl.BlockSpec((de...  19.2 us
    pallas_call x1, Pallas kernels, forward_legendre(): pl.pallas_call(functools.partial(forward_kernel, spans), grid_spec=pltpu....  16.8 us
  transfers between devices with their start and end apart: 3, of which 3 were waited for; matrix products, arithmetic and copies ran while one was open for 12% of the time, Pallas kernels for 6%

profile of v3, /device:TPU:1, one launch (start us, length us, event | category | flops | bytes accessed | tf_op | source)
XLA Modules:
  0.0 451.6 jit_solution(8239420499268385466)
XLA Ops:
  0.0 0.8 fusion.10.order_ref
  0.8 1.3 dynamic_slice.3.low_ref
  2.1 15.4 %inverse_legendre.1 = (bf16[16,16,40,256]{3,2,1,0:T(8,128)(2,1)}, bf16[16,4,40,256]{3,2,1,0:T(8,128)(2,1)}) custom-call(s32[20]{0:T(128)} %dynamic_slice.3.low_ref, bf16[20,641,256]{2,1,0:T(8,128)(2,1)} %spectral_ref.1, bf16[20,320,641]{2,1,0:T(8,128)(2,1)} %bitcast.13, bf16[256,256]{1,0:T(8,128)(2,1)} %fusion.10.order_ref), custom_call_target="tpu_custom_call" | custom-call | flops 4200857600 | bytes 21332480 | tf_op jit(solution)/shard_map/inverse_legendre/pallas_call | solution.py:189
  17.4 0.0 copy-start.5
  17.4 0.0 copy-start.4
  17.4 7.5 %all-to-all-start = ((bf16[16,16,40,256]{3,2,1,0:T(8,128)(2,1)}), bf16[16,16,40,256]{3,2,1,0:T(8,128)(2,1)}, u32[]{:S(2)}, u32[]{:S(2)}) async-start(bf16[16,16,40,256]{3,2,1,0:T(8,128)(2,1)} %get-tuple-element.28), calls=%async_computation | async-start | bytes 10485760 | tf_op jit(solution)/shard_map/all_to_all | solution.py:499
  24.9 0.0 copy-done.5
  25.0 0.1 copy.8
  25.1 0.1 reshape.161
  25.2 0.0 copy-done.4
  25.4 4.6 %reduce-window.6 = s32[1,16,25,128]{3,2,1,0:T(8,128)S(1)} reduce-window(s32[1,16,25,128]{3,2,1,0:T(8,128)S(1)} %reshape.169, s32[]{:T(128)} %constant.69.clone.1), window={size=1x1x1x128 pad=0_0x0_0x0_0x127_0}, to_apply=%region_0.1 | reduce-window | flops 6502400 | bytes 409604 | tf_op jit(solution)/shard_map/reduce-window
  30.0 0.5 slice_reduce_fusion
  30.5 0.2 reduce-window.9
  30.7 0.1 broadcast.148
  30.9 0.1 fusion.11
  31.0 15.0 %multiply_convert_fusion.1 = (bf16[640,1280]{1,0:T(8,128)(2,1)S(1)}, bf16[640,1280]{1,0:T(8,128)(2,1)S(1)}) fusion(s32[640]{0:T(1024)S(1)} %reshape.161), kind=kLoop, calls=%fused_computation.13 | loop fusion | flops 10649600 | bytes 3279360 | tf_op jit(solution)/shard_map/convert.2
  46.0 13.9 %multiply_convert_fusion.3 = (bf16[1280,640]{1,0:T(8,128)(2,1)S(1)}, bf16[1280,640]{1,0:T(8,128)(2,1)S(1)}) fusion(s32[640]{0:T(1024)S(1)} %reshape.161, f32[640]{0:T(1024)S(1)} %get-tuple-element.51, f32[640]{0:T(1024)S(1)} %get-tuple-element.52), kind=kLoop, calls=%fused_computation.18 | loop fusion | flops 10649600 | bytes 3284480 | tf_op jit(solution)/shard_map/convert.4
  59.9 5.7 %pad_maximum_fusion = (bf16[1280,1280]{1,0:T(8,128)(2,1)}, bf16[1280,1280]{1,0:T(8,128)(2,1)}) fusion(bf16[1280,640]{1,0:T(8,128)(2,1)S(1)} %get-tuple-element.50, bf16[1280,640]{1,0:T(8,128)(2,1)S(1)} %get-tuple-element.49, bf16[640,1280]{1,0:T(8,128)(2,1)S(1)} %get-tuple-element.48, bf16[640,1280]{1,0:T(8,128)(2,1)S(1)} %get-tuple-element.47), kind=kLoop, calls=%fused_computation.10 | loop fusion | flops 13107200 | bytes 13107200 | tf_op jit(solution)/shard_map/concatenate | solution.py:492
  65.6 55.7 %all-to-all-done.coeff_ref = bf16[16,16,40,256]{3,2,1,0:T(8,128)(2,1)} async-done(((bf16[16,16,40,256]{3,2,1,0:T(8,128)(2,1)}), bf16[16,16,40,256]{3,2,1,0:T(8,128)(2,1)}, u32[]{:S(2)}, u32[]{:S(2)}) %all-to-all-start) | async-done | bytes 5242912 | tf_op jit(solution)/shard_map/all_to_all | solution.py:499
  121.3 23.3 %all-to-all-start.1 = ((bf16[16,4,40,256]{3,2,1,0:T(8,128)(2,1)}), bf16[16,4,40,256]{3,2,1,0:T(8,128)(2,1)S(1)}, u32[]{:S(2)}, u32[]{:S(2)}) async-start(bf16[16,4,40,256]{3,2,1,0:T(8,128)(2,1)} %get-tuple-element.35), calls=%async_computation.1 | async-start | bytes 2621440 | tf_op jit(solution)/shard_map/all_to_all | solution.py:499
  144.6 13.8 %to_grid.2 = (f32[16,1280,128]{2,1,0:T(8,128)}, bf16[2560,128]{1,0:T(8,128)(2,1)}) custom-call(bf16[16,16,40,256]{3,2,1,0:T(8,128)(2,1)} %all-to-all-done.coeff_ref, bf16[1280,1280]{1,0:T(8,128)(2,1)} %get-tuple-element.43.table_ref), custom_call_target="tpu_custom_call" | custom-call | flops 6710886400 | bytes 8519680 | tf_op jit(solution)/shard_map/to_grid/pallas_call | solution.py:246
  158.4 0.2 broadcast_in_dim.29
  158.6 8.4 %scatter_fusion = bf16[6400,128]{1,0:T(8,128)(2,1)S(1)} fusion(bf16[6400,128]{1,0:T(8,128)(2,1)S(1)} %broadcast_in_dim.29, s32[2560]{0:T(1024)S(1)} %compare_select_fusion.1, bf16[2560,128]{1,0:T(8,128)(2,1)} %get-tuple-element.39), kind=kCustom, calls=%fused_computation.2 | custom fusion | bytes 1976320 | tf_op jit(solution)/shard_map/scatter | solution.py:544
  167.0 5.4 %all-to-all-done.1.coeff_ref = bf16[16,4,40,256]{3,2,1,0:T(8,128)(2,1)S(1)} async-done(((bf16[16,4,40,256]{3,2,1,0:T(8,128)(2,1)}), bf16[16,4,40,256]{3,2,1,0:T(8,128)(2,1)S(1)}, u32[]{:S(2)}, u32[]{:S(2)}) %all-to-all-start.1) | async-done | bytes 1310752 | tf_op jit(solution)/shard_map/all_to_all | solution.py:499
  172.5 0.0 copy-start.3
  172.5 1.1 copy-done.3
  173.5 5.5 %to_grid.3 = (f32[4,1280,128]{2,1,0:T(8,128)}, bf16[640,128]{1,0:T(8,128)(2,1)}) custom-call(bf16[16,4,40,256]{3,2,1,0:T(8,128)(2,1)} %copy-done.3, bf16[1280,1280]{1,0:T(8,128)(2,1)} %get-tuple-element.43.table_ref), custom_call_target="tpu_custom_call" | custom-call | flops 1677721600 | bytes 4587520 | tf_op jit(solution)/shard_map/to_grid/pallas_call | solution.py:246
  179.0 5.5 %scatter_fusion.1 = bf16[6400,128]{1,0:T(8,128)(2,1)S(1)} fusion(bf16[6400,128]{1,0:T(8,128)(2,1)S(1)} %scatter_fusion, s32[640]{0:T(1024)S(1)} %compare_select_fusion.2, bf16[640,128]{1,0:T(8,128)(2,1)} %get-tuple-element.44), kind=kCustom, calls=%fused_computation.3 | custom fusion | bytes 494080 | tf_op jit(solution)/shard_map/scatter | solution.py:544
  184.6 0.0 copy-start
  184.6 1.2 copy-done
  185.8 83.7 %network.1 = bf16[16,400,128]{2,1,0:T(8,128)(2,1)} custom-call(bf16[16,400,128]{2,1,0:T(8,128)(2,1)} %bitcast.12, bf16[1,128,1024]{2,1,0:T(8,128)(2,1)} %in_ref.1, bf16[1,1024,1024]{2,1,0:T(8,128)(2,1)} %mid_ref.1, bf16[1,1024,128]{2,1,0:T(8,128)(2,1)} %out_ref.1), custom_call_target="tpu_custom_call" | custom-call | flops 16777216000 | bytes 5373952 | tf_op jit(solution)/shard_map/network/pallas_call | solution.py:466
  269.5 3.9 gather_fusion.1
  273.4 0.0 copy-start.1
  273.4 5.6 %to_fourier.3 = bf16[16,4,40,256]{3,2,1,0:T(8,128)(2,1)} custom-call(f32[4,1280,128]{2,1,0:T(8,128)} %get-tuple-element.46.forced_ref, bf16[640,128]{1,0:T(8,128)(2,1)} %gather_fusion.1, bf16[1280,1280]{1,0:T(8,128)(2,1)} %get-tuple-element.45.table_ref), custom_call_target="tpu_custom_call" | custom-call | flops 1677721600 | bytes 5898240 | tf_op jit(solution)/shard_map/to_fourier/pallas_call | solution.py:299
  279.0 5.3 %all-to-all-start.3 = ((bf16[16,4,40,256]{3,2,1,0:T(8,128)(2,1)}), bf16[16,4,40,256]{3,2,1,0:T(8,128)(2,1)S(1)}, u32[]{:S(2)}, u32[]{:S(2)}) async-start(bf16[16,4,40,256]{3,2,1,0:T(8,128)(2,1)} %to_fourier.3), calls=%async_computation.3 | async-start | bytes 2621440 | tf_op jit(solution)/shard_map/all_to_all | solution.py:499
  284.3 0.0 copy-done.1
  284.3 6.1 %gather_fusion = bf16[2560,128]{1,0:T(8,128)(2,1)} fusion(bf16[6400,128]{1,0:T(8,128)(2,1)S(1)} %bitcast.16, s32[3072]{0:T(1024)S(1)} %pad_clamp_fusion), kind=kCustom, calls=%fused_computation | custom fusion | bytes 1320960 | tf_op jit(solution)/shard_map/gather | solution.py:551
  290.4 14.1 %to_fourier.2 = bf16[16,16,40,256]{3,2,1,0:T(8,128)(2,1)} custom-call(f32[16,1280,128]{2,1,0:T(8,128)} %get-tuple-element.34.forced_ref, bf16[2560,128]{1,0:T(8,128)(2,1)} %gather_fusion, bf16[1280,1280]{1,0:T(8,128)(2,1)} %get-tuple-element.45.table_ref), custom_call_target="tpu_custom_call" | custom-call | flops 6710886400 | bytes 13762560 | tf_op jit(solution)/shard_map/to_fourier/pallas_call | solution.py:299
  304.5 7.6 %all-to-all-done.3.rest_1_ = bf16[16,4,40,256]{3,2,1,0:T(8,128)(2,1)S(1)} async-done(((bf16[16,4,40,256]{3,2,1,0:T(8,128)(2,1)}), bf16[16,4,40,256]{3,2,1,0:T(8,128)(2,1)S(1)}, u32[]{:S(2)}, u32[]{:S(2)}) %all-to-all-start.3) | async-done | bytes 1310752 | tf_op jit(solution)/shard_map/all_to_all | solution.py:499
  312.1 0.0 copy-start.2
  312.1 122.7 %all_to_all.20.rest_0_ = bf16[16,16,40,256]{3,2,1,0:T(8,128)(2,1)} all-to-all(bf16[16,16,40,256]{3,2,1,0:T(8,128)(2,1)} %to_fourier.2), channel_id=1, replica_groups=mesh['grp'=2,'wave'=16] {'wave'}, dimensions={0} | all-to-all | bytes 10485760 | tf_op jit(solution)/shard_map/all_to_all | solution.py:499
  434.8 0.0 copy-done.2
  434.8 16.8 %forward_legendre.1 = bf16[20,641,256]{2,1,0:T(8,128)(2,1)} custom-call(s32[20]{0:T(128)} %dynamic_slice.3.low_ref, bf16[20,320,641]{2,1,0:T(8,128)(2,1)} %bitcast.14, bf16[256,256]{1,0:T(8,128)(2,1)} %fusion.10.order_ref, bf16[16,16,40,256]{3,2,1,0:T(8,128)(2,1)} %all_to_all.20.rest_0_, bf16[16,4,40,256]{3,2,1,0:T(8,128)(2,1)} %copy-done.2), custom_call_target="tpu_custom_call" | custom-call | flops 4200857600 | bytes 16409600 | tf_op jit(solution)/shard_map/forward_legendre/pallas_call | solution.py:365
  (18 shorter events, 0.3 us)
Async XLA Ops:
  17.4 7.5 %copy-start.5 = (s32[320]{0:T(512)S(1)}, s32[320]{0:T(512)}, u32[]{:S(2)}) copy-start(s32[320]{0:T(512)} %param.9) | copy-start | bytes 3844
  17.4 7.8 %copy-start.4 = (s32[3200,1]{0,1:T(1,128)S(1)}, s32[3200,1]{0,1:T(1,128)}, u32[]{:S(2)}) copy-start(s32[3200,1]{0,1:T(1,128)} %param.10) | copy-start | bytes 38404
  17.4 103.9 %all-to-all-start = ((bf16[16,16,40,256]{3,2,1,0:T(8,128)(2,1)}), bf16[16,16,40,256]{3,2,1,0:T(8,128)(2,1)}, u32[]{:S(2)}, u32[]{:S(2)}) async-start(bf16[16,16,40,256]{3,2,1,0:T(8,128)(2,1)} %get-tuple-element.28), calls=%async_computation | async-start | bytes 10485760 | tf_op jit(solution)/shard_map/all_to_all | solution.py:499
  121.3 51.1 %all-to-all-start.1 = ((bf16[16,4,40,256]{3,2,1,0:T(8,128)(2,1)}), bf16[16,4,40,256]{3,2,1,0:T(8,128)(2,1)S(1)}, u32[]{:S(2)}, u32[]{:S(2)}) async-start(bf16[16,4,40,256]{3,2,1,0:T(8,128)(2,1)} %get-tuple-element.35), calls=%async_computation.1 | async-start | bytes 2621440 | tf_op jit(solution)/shard_map/all_to_all | solution.py:499
  172.5 1.1 copy-start.3
  184.6 1.2 copy-start
  273.4 10.9 %copy-start.1 = (bf16[16,400,128]{2,1,0:T(8,128)(2,1)S(1)}, bf16[16,400,128]{2,1,0:T(8,128)(2,1)}, u32[]{:S(2)}) copy-start(bf16[16,400,128]{2,1,0:T(8,128)(2,1)} %network.1) | copy-start | bytes 4915204
  279.0 33.2 %all-to-all-start.3 = ((bf16[16,4,40,256]{3,2,1,0:T(8,128)(2,1)}), bf16[16,4,40,256]{3,2,1,0:T(8,128)(2,1)S(1)}, u32[]{:S(2)}, u32[]{:S(2)}) async-start(bf16[16,4,40,256]{3,2,1,0:T(8,128)(2,1)} %to_fourier.3), calls=%async_computation.3 | async-start | bytes 2621440 | tf_op jit(solution)/shard_map/all_to_all | solution.py:499
  312.1 122.7 %copy-start.2 = (bf16[16,4,40,256]{3,2,1,0:T(8,128)(2,1)}, bf16[16,4,40,256]{3,2,1,0:T(8,128)(2,1)S(1)}, u32[]{:S(2)}) copy-start(bf16[16,4,40,256]{3,2,1,0:T(8,128)(2,1)S(1)} %all-to-all-done.3.rest_1_) | copy-start | bytes 3932164

commit v4 on v3

--- a/solution.py
+++ b/solution.py
@@ -399,7 +399,10 @@
     barrier = pltpu.get_barrier_semaphore()
 
     def peer(k):
-        return lax.rem(me + k, devices)
+        other = 0
+        for bit in range(devices.bit_length() - 1):
+            other = other + (me // (1 << bit) + k // (1 << bit)) % 2 * (1 << bit)
+        return other
 
     def outward(k, source, target):
         return pltpu.make_async_remote_copy(
@@ -417,7 +420,7 @@
             dst_ref=result_ref.at[owner],
             send_sem=backs.at[k],
             recv_sem=returns.at[k],
-            device_id={"wave": peer(devices - k)},
+            device_id={"wave": peer(k)},
             device_id_type=pl.DeviceIdType.MESH,
         )
 
@@ -436,12 +439,14 @@
         )
         return carry
 
-    def send(k, carry):
+    def send(i, carry):
+        k = devices - i
         outward(k, me, peer(k)).start()
         return carry
 
-    def serve(k, carry):
-        source = peer(devices - k)
+    def serve(i, carry):
+        k = devices - i
+        source = peer(k)
         outward(k, source, peer(k)).wait_recv()
         answers[source] = answer(arrived[source])
         backward(k, source, me).start()
@@ -449,7 +454,7 @@
 
     def finish(k, carry):
         outward(k, me, peer(k)).wait_send()
-        backward(k, peer(devices - k), me).wait_send()
+        backward(k, peer(k), me).wait_send()
         backward(k, peer(k), peer(k)).wait_recv()
         return carry
 
@@ -560,6 +565,7 @@
         and 2 * spectral.shape[0] % 8 == 0
         and legendre.shape[2] // devices % 2 == 0
         and 2 * routes.shape[0] // devices % 8 == 0
+        and devices & (devices - 1) == 0
     )
     body = on_device_kernels if aligned else on_device_arrays
     return body(spectral, legendre, pair_low, routes, w_in, w_mid, w_out)

time: 453 us -> 452 us (level)
  no operation moved by 1% of the time
where the time goes in v4:
time: 452 us; the launch traced here: 451 us
  Pallas kernels  155 us (34%)
  blocking collectives  123 us (27%)
  waiting for transfers between devices  68.7 us (15%)
  other arithmetic  40.4 us (9%)
  starting transfers between devices  35.5 us (8%)
  local copies, waits for them, and re-layouts  28.8 us (6%)
    all_to_all x1, blocking collectives, exchange(): lax.all_to_all(values, 'wave', split_axis=0, concat_axis=0, tiled=True)  123 us
    pallas_call x1, Pallas kernels, run_network(): pl.pallas_call(network_kernel, in_specs=[pl.BlockSpec(memory_space=pltpu....  83.6 us
    all_to_all x3, waiting for transfers between devices, exchange(): lax.all_to_all(values, 'wave', split_axis=0, concat_axis=0, tiled=True)  68.7 us
    all_to_all x3, starting transfers between devices, exchange(): lax.all_to_all(values, 'wave', split_axis=0, concat_axis=0, tiled=True)  35.5 us
    another operation x5, other arithmetic  33.8 us
    pallas_call x2, Pallas kernels, to_fourier(): pl.pallas_call(fourier_kernel, grid=(lats // 2,), in_specs=[pl.BlockSpec(...  19.7 us
    pallas_call x2, Pallas kernels, to_grid(): pl.pallas_call(grid_kernel, grid=(lats // 2,), in_specs=[pl.BlockSpec((de...  19.2 us
    pallas_call x1, Pallas kernels, forward_legendre(): pl.pallas_call(functools.partial(forward_kernel, spans), grid_spec=pltpu....  16.8 us
  transfers between devices with their start and end apart: 3, of which 3 were waited for; matrix products, arithmetic and copies ran while one was open for 12% of the time, Pallas kernels for 6%

profile of v4, /device:TPU:1, one launch (start us, length us, event | category | flops | bytes accessed | tf_op | source)
XLA Modules:
  0.0 450.9 jit_solution(3460164439048343164)
XLA Ops:
  0.0 0.8 fusion.10.order_ref
  0.8 1.3 dynamic_slice.3.low_ref
  2.1 15.4 %inverse_legendre.1 = (bf16[16,16,40,256]{3,2,1,0:T(8,128)(2,1)}, bf16[16,4,40,256]{3,2,1,0:T(8,128)(2,1)}) custom-call(s32[20]{0:T(128)} %dynamic_slice.3.low_ref, bf16[20,641,256]{2,1,0:T(8,128)(2,1)} %spectral_ref.1, bf16[20,320,641]{2,1,0:T(8,128)(2,1)} %bitcast.13, bf16[256,256]{1,0:T(8,128)(2,1)} %fusion.10.order_ref), custom_call_target="tpu_custom_call" | custom-call | flops 4200857600 | bytes 21332480 | tf_op jit(solution)/shard_map/inverse_legendre/pallas_call | solution.py:189
  17.4 0.0 copy-start.5
  17.4 0.0 copy-start.4
  17.4 7.5 %all-to-all-start = ((bf16[16,16,40,256]{3,2,1,0:T(8,128)(2,1)}), bf16[16,16,40,256]{3,2,1,0:T(8,128)(2,1)}, u32[]{:S(2)}, u32[]{:S(2)}) async-start(bf16[16,16,40,256]{3,2,1,0:T(8,128)(2,1)} %get-tuple-element.28), calls=%async_computation | async-start | bytes 10485760 | tf_op jit(solution)/shard_map/all_to_all | solution.py:504
  24.9 0.0 copy-done.5
  25.0 0.1 copy.8
  25.1 0.1 reshape.161
  25.2 0.0 copy-done.4
  25.4 4.6 %reduce-window.6 = s32[1,16,25,128]{3,2,1,0:T(8,128)S(1)} reduce-window(s32[1,16,25,128]{3,2,1,0:T(8,128)S(1)} %reshape.169, s32[]{:T(128)} %constant.69.clone.1), window={size=1x1x1x128 pad=0_0x0_0x0_0x127_0}, to_apply=%region_0.1 | reduce-window | flops 6502400 | bytes 409604 | tf_op jit(solution)/shard_map/reduce-window
  30.0 0.5 slice_reduce_fusion
  30.5 0.2 reduce-window.9
  30.7 0.1 broadcast.148
  30.9 0.1 fusion.11
  31.0 15.0 %multiply_convert_fusion.1 = (bf16[640,1280]{1,0:T(8,128)(2,1)S(1)}, bf16[640,1280]{1,0:T(8,128)(2,1)S(1)}) fusion(s32[640]{0:T(1024)S(1)} %reshape.161), kind=kLoop, calls=%fused_computation.13 | loop fusion | flops 10649600 | bytes 3279360 | tf_op jit(solution)/shard_map/convert.2
  46.0 13.9 %multiply_convert_fusion.3 = (bf16[1280,640]{1,0:T(8,128)(2,1)S(1)}, bf16[1280,640]{1,0:T(8,128)(2,1)S(1)}) fusion(s32[640]{0:T(1024)S(1)} %reshape.161, f32[640]{0:T(1024)S(1)} %get-tuple-element.51, f32[640]{0:T(1024)S(1)} %get-tuple-element.52), kind=kLoop, calls=%fused_computation.18 | loop fusion | flops 10649600 | bytes 3284480 | tf_op jit(solution)/shard_map/convert.4
  59.9 5.7 %pad_maximum_fusion = (bf16[1280,1280]{1,0:T(8,128)(2,1)}, bf16[1280,1280]{1,0:T(8,128)(2,1)}) fusion(bf16[1280,640]{1,0:T(8,128)(2,1)S(1)} %get-tuple-element.50, bf16[1280,640]{1,0:T(8,128)(2,1)S(1)} %get-tuple-element.49, bf16[640,1280]{1,0:T(8,128)(2,1)S(1)} %get-tuple-element.48, bf16[640,1280]{1,0:T(8,128)(2,1)S(1)} %get-tuple-element.47), kind=kLoop, calls=%fused_computation.10 | loop fusion | flops 13107200 | bytes 13107200 | tf_op jit(solution)/shard_map/concatenate | solution.py:497
  65.6 55.7 %all-to-all-done.coeff_ref = bf16[16,16,40,256]{3,2,1,0:T(8,128)(2,1)} async-done(((bf16[16,16,40,256]{3,2,1,0:T(8,128)(2,1)}), bf16[16,16,40,256]{3,2,1,0:T(8,128)(2,1)}, u32[]{:S(2)}, u32[]{:S(2)}) %all-to-all-start) | async-done | bytes 5242912 | tf_op jit(solution)/shard_map/all_to_all | solution.py:504
  121.3 23.3 %all-to-all-start.1 = ((bf16[16,4,40,256]{3,2,1,0:T(8,128)(2,1)}), bf16[16,4,40,256]{3,2,1,0:T(8,128)(2,1)S(1)}, u32[]{:S(2)}, u32[]{:S(2)}) async-start(bf16[16,4,40,256]{3,2,1,0:T(8,128)(2,1)} %get-tuple-element.35), calls=%async_computation.1 | async-start | bytes 2621440 | tf_op jit(solution)/shard_map/all_to_all | solution.py:504
  144.6 13.8 %to_grid.2 = (f32[16,1280,128]{2,1,0:T(8,128)}, bf16[2560,128]{1,0:T(8,128)(2,1)}) custom-call(bf16[16,16,40,256]{3,2,1,0:T(8,128)(2,1)} %all-to-all-done.coeff_ref, bf16[1280,1280]{1,0:T(8,128)(2,1)} %get-tuple-element.43.table_ref), custom_call_target="tpu_custom_call" | custom-call | flops 6710886400 | bytes 8519680 | tf_op jit(solution)/shard_map/to_grid/pallas_call | solution.py:246
  158.4 0.2 broadcast_in_dim.29
  158.6 8.4 %scatter_fusion = bf16[6400,128]{1,0:T(8,128)(2,1)S(1)} fusion(bf16[6400,128]{1,0:T(8,128)(2,1)S(1)} %broadcast_in_dim.29, s32[2560]{0:T(1024)S(1)} %compare_select_fusion.1, bf16[2560,128]{1,0:T(8,128)(2,1)} %get-tuple-element.39), kind=kCustom, calls=%fused_computation.2 | custom fusion | bytes 1976320 | tf_op jit(solution)/shard_map/scatter | solution.py:549
  167.0 5.4 %all-to-all-done.1.coeff_ref = bf16[16,4,40,256]{3,2,1,0:T(8,128)(2,1)S(1)} async-done(((bf16[16,4,40,256]{3,2,1,0:T(8,128)(2,1)}), bf16[16,4,40,256]{3,2,1,0:T(8,128)(2,1)S(1)}, u32[]{:S(2)}, u32[]{:S(2)}) %all-to-all-start.1) | async-done | bytes 1310752 | tf_op jit(solution)/shard_map/all_to_all | solution.py:504
  172.5 0.0 copy-start.3
  172.5 1.1 copy-done.3
  173.5 5.5 %to_grid.3 = (f32[4,1280,128]{2,1,0:T(8,128)}, bf16[640,128]{1,0:T(8,128)(2,1)}) custom-call(bf16[16,4,40,256]{3,2,1,0:T(8,128)(2,1)} %copy-done.3, bf16[1280,1280]{1,0:T(8,128)(2,1)} %get-tuple-element.43.table_ref), custom_call_target="tpu_custom_call" | custom-call | flops 1677721600 | bytes 4587520 | tf_op jit(solution)/shard_map/to_grid/pallas_call | solution.py:246
  179.0 5.5 %scatter_fusion.1 = bf16[6400,128]{1,0:T(8,128)(2,1)S(1)} fusion(bf16[6400,128]{1,0:T(8,128)(2,1)S(1)} %scatter_fusion, s32[640]{0:T(1024)S(1)} %compare_select_fusion.2, bf16[640,128]{1,0:T(8,128)(2,1)} %get-tuple-element.44), kind=kCustom, calls=%fused_computation.3 | custom fusion | bytes 494080 | tf_op jit(solution)/shard_map/scatter | solution.py:549
  184.6 0.0 copy-start
  184.6 1.2 copy-done
  185.8 83.6 %network.1 = bf16[16,400,128]{2,1,0:T(8,128)(2,1)} custom-call(bf16[16,400,128]{2,1,0:T(8,128)(2,1)} %bitcast.12, bf16[1,128,1024]{2,1,0:T(8,128)(2,1)} %in_ref.1, bf16[1,1024,1024]{2,1,0:T(8,128)(2,1)} %mid_ref.1, bf16[1,1024,128]{2,1,0:T(8,128)(2,1)} %out_ref.1), custom_call_target="tpu_custom_call" | custom-call | flops 16777216000 | bytes 5373952 | tf_op jit(solution)/shard_map/network/pallas_call | solution.py:471
  269.4 3.9 gather_fusion.1
  273.3 0.0 copy-start.1
  273.3 5.6 %to_fourier.3 = bf16[16,4,40,256]{3,2,1,0:T(8,128)(2,1)} custom-call(f32[4,1280,128]{2,1,0:T(8,128)} %get-tuple-element.46.forced_ref, bf16[640,128]{1,0:T(8,128)(2,1)} %gather_fusion.1, bf16[1280,1280]{1,0:T(8,128)(2,1)} %get-tuple-element.45.table_ref), custom_call_target="tpu_custom_call" | custom-call | flops 1677721600 | bytes 5898240 | tf_op jit(solution)/shard_map/to_fourier/pallas_call | solution.py:299
  278.8 4.7 %all-to-all-start.3 = ((bf16[16,4,40,256]{3,2,1,0:T(8,128)(2,1)}), bf16[16,4,40,256]{3,2,1,0:T(8,128)(2,1)S(1)}, u32[]{:S(2)}, u32[]{:S(2)}) async-start(bf16[16,4,40,256]{3,2,1,0:T(8,128)(2,1)} %to_fourier.3), calls=%async_computation.3 | async-start | bytes 2621440 | tf_op jit(solution)/shard_map/all_to_all | solution.py:504
  283.6 0.0 copy-done.1
  283.6 6.1 %gather_fusion = bf16[2560,128]{1,0:T(8,128)(2,1)} fusion(bf16[6400,128]{1,0:T(8,128)(2,1)S(1)} %bitcast.16, s32[3072]{0:T(1024)S(1)} %pad_clamp_fusion), kind=kCustom, calls=%fused_computation | custom fusion | bytes 1320960 | tf_op jit(solution)/shard_map/gather | solution.py:556
  289.7 14.1 %to_fourier.2 = bf16[16,16,40,256]{3,2,1,0:T(8,128)(2,1)} custom-call(f32[16,1280,128]{2,1,0:T(8,128)} %get-tuple-element.34.forced_ref, bf16[2560,128]{1,0:T(8,128)(2,1)} %gather_fusion, bf16[1280,1280]{1,0:T(8,128)(2,1)} %get-tuple-element.45.table_ref), custom_call_target="tpu_custom_call" | custom-call | flops 6710886400 | bytes 13762560 | tf_op jit(solution)/shard_map/to_fourier/pallas_call | solution.py:299
  303.8 7.6 %all-to-all-done.3.rest_1_ = bf16[16,4,40,256]{3,2,1,0:T(8,128)(2,1)S(1)} async-done(((bf16[16,4,40,256]{3,2,1,0:T(8,128)(2,1)}), bf16[16,4,40,256]{3,2,1,0:T(8,128)(2,1)S(1)}, u32[]{:S(2)}, u32[]{:S(2)}) %all-to-all-start.3) | async-done | bytes 1310752 | tf_op jit(solution)/shard_map/all_to_all | solution.py:504
  311.4 0.0 copy-start.2
  311.4 122.7 %all_to_all.20.rest_0_ = bf16[16,16,40,256]{3,2,1,0:T(8,128)(2,1)} all-to-all(bf16[16,16,40,256]{3,2,1,0:T(8,128)(2,1)} %to_fourier.2), channel_id=1, replica_groups=mesh['grp'=2,'wave'=16] {'wave'}, dimensions={0} | all-to-all | bytes 10485760 | tf_op jit(solution)/shard_map/all_to_all | solution.py:504
  434.1 0.0 copy-done.2
  434.1 16.8 %forward_legendre.1 = bf16[20,641,256]{2,1,0:T(8,128)(2,1)} custom-call(s32[20]{0:T(128)} %dynamic_slice.3.low_ref, bf16[20,320,641]{2,1,0:T(8,128)(2,1)} %bitcast.14, bf16[256,256]{1,0:T(8,128)(2,1)} %fusion.10.order_ref, bf16[16,16,40,256]{3,2,1,0:T(8,128)(2,1)} %all_to_all.20.rest_0_, bf16[16,4,40,256]{3,2,1,0:T(8,128)(2,1)} %copy-done.2), custom_call_target="tpu_custom_call" | custom-call | flops 4200857600 | bytes 16409600 | tf_op jit(solution)/shard_map/forward_legendre/pallas_call | solution.py:365
  (18 shorter events, 0.3 us)
Async XLA Ops:
  17.4 7.5 %copy-start.5 = (s32[320]{0:T(512)S(1)}, s32[320]{0:T(512)}, u32[]{:S(2)}) copy-start(s32[320]{0:T(512)} %param.9) | copy-start | bytes 3844
  17.4 7.8 %copy-start.4 = (s32[3200,1]{0,1:T(1,128)S(1)}, s32[3200,1]{0,1:T(1,128)}, u32[]{:S(2)}) copy-start(s32[3200,1]{0,1:T(1,128)} %param.10) | copy-start | bytes 38404
  17.4 103.9 %all-to-all-start = ((bf16[16,16,40,256]{3,2,1,0:T(8,128)(2,1)}), bf16[16,16,40,256]{3,2,1,0:T(8,128)(2,1)}, u32[]{:S(2)}, u32[]{:S(2)}) async-start(bf16[16,16,40,256]{3,2,1,0:T(8,128)(2,1)} %get-tuple-element.28), calls=%async_computation | async-start | bytes 10485760 | tf_op jit(solution)/shard_map/all_to_all | solution.py:504
  121.3 51.1 %all-to-all-start.1 = ((bf16[16,4,40,256]{3,2,1,0:T(8,128)(2,1)}), bf16[16,4,40,256]{3,2,1,0:T(8,128)(2,1)S(1)}, u32[]{:S(2)}, u32[]{:S(2)}) async-start(bf16[16,4,40,256]{3,2,1,0:T(8,128)(2,1)} %get-tuple-element.35), calls=%async_computation.1 | async-start | bytes 2621440 | tf_op jit(solution)/shard_map/all_to_all | solution.py:504
  172.5 1.1 copy-start.3
  184.6 1.2 copy-start
  273.3 10.3 %copy-start.1 = (bf16[16,400,128]{2,1,0:T(8,128)(2,1)S(1)}, bf16[16,400,128]{2,1,0:T(8,128)(2,1)}, u32[]{:S(2)}) copy-start(bf16[16,400,128]{2,1,0:T(8,128)(2,1)} %network.1) | copy-start | bytes 4915204
  278.8 32.5 %all-to-all-start.3 = ((bf16[16,4,40,256]{3,2,1,0:T(8,128)(2,1)}), bf16[16,4,40,256]{3,2,1,0:T(8,128)(2,1)S(1)}, u32[]{:S(2)}, u32[]{:S(2)}) async-start(bf16[16,4,40,256]{3,2,1,0:T(8,128)(2,1)} %to_fourier.3), calls=%async_computation.3 | async-start | bytes 2621440 | tf_op jit(solution)/shard_map/all_to_all | solution.py:504
  311.4 122.7 %copy-start.2 = (bf16[16,4,40,256]{3,2,1,0:T(8,128)(2,1)}, bf16[16,4,40,256]{3,2,1,0:T(8,128)(2,1)S(1)}, u32[]{:S(2)}) copy-start(bf16[16,4,40,256]{3,2,1,0:T(8,128)(2,1)S(1)} %all-to-all-done.3.rest_1_) | copy-start | bytes 3932164

commit v5 on v4

--- a/solution.py
+++ b/solution.py
@@ -506,7 +506,7 @@
 
 def row_spans(lat_rows):
     pairs = lat_rows // 2
-    first = max(1, pairs * 4 // 5)
+    first = max(1, pairs * 9 // 10)
     spans = [(0, 2 * first), (2 * first, 2 * (pairs - first))]
     return [span for span in spans if span[1] > 0]
 

time: 452 us -> 469 us (1.038)
  blocking collectives: 123 us -> 137 us
    all_to_all x1, blocking collectives: 123 us -> 137 us  [exchange(): lax.all_to_all(values, 'wave', split_axis=0, concat_axis=0, tiled=True)]
  transfers between devices with their start and end apart: 3 -> 3, of which waited for: 3 -> 1; matrix products, arithmetic and copies ran while one was open for 12% -> 13% of each run, Pallas kernels for 6% -> 7%
where the time goes in v5:
time: 469 us; the launch traced here: 467 us
  Pallas kernels  154 us (33%)
  blocking collectives  137 us (29%)
  waiting for transfers between devices  67.2 us (14%)
  other arithmetic  40.4 us (9%)
  starting transfers between devices  38.4 us (8%)
  local copies, waits for them, and re-layouts  30.4 us (6%)
    all_to_all x1, blocking collectives, exchange(): lax.all_to_all(values, 'wave', split_axis=0, concat_axis=0, tiled=True)  137 us
    pallas_call x1, Pallas kernels, run_network(): pl.pallas_call(network_kernel, in_specs=[pl.BlockSpec(memory_space=pltpu....  82.5 us
    all_to_all x3, waiting for transfers between devices, exchange(): lax.all_to_all(values, 'wave', split_axis=0, concat_axis=0, tiled=True)  67.2 us
    all_to_all x3, starting transfers between devices, exchange(): lax.all_to_all(values, 'wave', split_axis=0, concat_axis=0, tiled=True)  38.4 us
    another operation x5, other arithmetic  33.8 us
    pallas_call x2, Pallas kernels, to_fourier(): pl.pallas_call(fourier_kernel, grid=(lats // 2,), in_specs=[pl.BlockSpec(...  19.9 us
    pallas_call x2, Pallas kernels, to_grid(): pl.pallas_call(grid_kernel, grid=(lats // 2,), in_specs=[pl.BlockSpec((de...  19.6 us
    pallas_call x1, Pallas kernels, forward_legendre(): pl.pallas_call(functools.partial(forward_kernel, spans), grid_spec=pltpu....  16.9 us
  transfers between devices with their start and end apart: 3, of which 1 were waited for; matrix products, arithmetic and copies ran while one was open for 13% of the time, Pallas kernels for 7%

profile of v5, /device:TPU:1, one launch (start us, length us, event | category | flops | bytes accessed | tf_op | source)
XLA Modules:
  0.0 467.3 jit_solution(3391056632604891354)
XLA Ops:
  0.0 0.8 fusion.10.order_ref
  0.8 1.3 dynamic_slice.3.low_ref
  2.0 15.3 %inverse_legendre.1 = (bf16[16,18,40,256]{3,2,1,0:T(8,128)(2,1)}, bf16[16,2,40,256]{3,2,1,0:T(8,128)(2,1)}) custom-call(s32[20]{0:T(128)} %dynamic_slice.3.low_ref, bf16[20,641,256]{2,1,0:T(8,128)(2,1)} %spectral_ref.1, bf16[20,320,641]{2,1,0:T(8,128)(2,1)} %bitcast.13, bf16[256,256]{1,0:T(8,128)(2,1)} %fusion.10.order_ref), custom_call_target="tpu_custom_call" | custom-call | flops 4200857600 | bytes 21332480 | tf_op jit(solution)/shard_map/inverse_legendre/pallas_call | solution.py:189
  17.4 0.0 copy-start.5
  17.4 0.0 copy-start.4
  17.4 7.5 %all-to-all-start = ((bf16[16,18,40,256]{3,2,1,0:T(8,128)(2,1)}), bf16[16,18,40,256]{3,2,1,0:T(8,128)(2,1)}, u32[]{:S(2)}, u32[]{:S(2)}) async-start(bf16[16,18,40,256]{3,2,1,0:T(8,128)(2,1)} %get-tuple-element.28), calls=%async_computation | async-start | bytes 11796480 | tf_op jit(solution)/shard_map/all_to_all | solution.py:504
  24.9 0.0 copy-done.5
  24.9 0.1 copy.8
  25.1 0.1 reshape.161
  25.2 0.0 copy-done.4
  25.4 4.6 reduce-window.6
  30.0 0.5 slice_reduce_fusion
  30.5 0.2 reduce-window.9
  30.7 0.1 broadcast.147
  30.9 0.1 fusion.11
  31.0 15.0 %multiply_convert_fusion.1 = (bf16[640,1280]{1,0:T(8,128)(2,1)S(1)}, bf16[640,1280]{1,0:T(8,128)(2,1)S(1)}) fusion(s32[640]{0:T(1024)S(1)} %reshape.161), kind=kLoop, calls=%fused_computation.13 | loop fusion | flops 10649600 | bytes 3279360 | tf_op jit(solution)/shard_map/convert.2
  46.0 13.9 %multiply_convert_fusion.3 = (bf16[1280,640]{1,0:T(8,128)(2,1)S(1)}, bf16[1280,640]{1,0:T(8,128)(2,1)S(1)}) fusion(s32[640]{0:T(1024)S(1)} %reshape.161, f32[640]{0:T(1024)S(1)} %get-tuple-element.51, f32[640]{0:T(1024)S(1)} %get-tuple-element.52), kind=kLoop, calls=%fused_computation.18 | loop fusion | flops 10649600 | bytes 3284480 | tf_op jit(solution)/shard_map/convert.4
  59.9 5.6 %pad_maximum_fusion = (bf16[1280,1280]{1,0:T(8,128)(2,1)}, bf16[1280,1280]{1,0:T(8,128)(2,1)}) fusion(bf16[1280,640]{1,0:T(8,128)(2,1)S(1)} %get-tuple-element.50, bf16[1280,640]{1,0:T(8,128)(2,1)S(1)} %get-tuple-element.49, bf16[640,1280]{1,0:T(8,128)(2,1)S(1)} %get-tuple-element.48, bf16[640,1280]{1,0:T(8,128)(2,1)S(1)} %get-tuple-element.47), kind=kLoop, calls=%fused_computation.10 | loop fusion | flops 13107200 | bytes 13107200 | tf_op jit(solution)/shard_map/concatenate | solution.py:497
  65.6 67.1 %all-to-all-done.coeff_ref = bf16[16,18,40,256]{3,2,1,0:T(8,128)(2,1)} async-done(((bf16[16,18,40,256]{3,2,1,0:T(8,128)(2,1)}), bf16[16,18,40,256]{3,2,1,0:T(8,128)(2,1)}, u32[]{:S(2)}, u32[]{:S(2)}) %all-to-all-start) | async-done | bytes 5898272 | tf_op jit(solution)/shard_map/all_to_all | solution.py:504
  132.7 25.9 %all-to-all-start.1 = ((bf16[16,2,40,256]{3,2,1,0:T(8,128)(2,1)}), bf16[16,2,40,256]{3,2,1,0:T(8,128)(2,1)S(1)}, u32[]{:S(2)}, u32[]{:S(2)}) async-start(bf16[16,2,40,256]{3,2,1,0:T(8,128)(2,1)} %get-tuple-element.35), calls=%async_computation.1 | async-start | bytes 1310720 | tf_op jit(solution)/shard_map/all_to_all | solution.py:504
  158.7 15.2 %to_grid.2 = (f32[18,1280,128]{2,1,0:T(8,128)}, bf16[2880,128]{1,0:T(8,128)(2,1)}) custom-call(bf16[16,18,40,256]{3,2,1,0:T(8,128)(2,1)} %all-to-all-done.coeff_ref, bf16[1280,1280]{1,0:T(8,128)(2,1)} %get-tuple-element.43.table_ref), custom_call_target="tpu_custom_call" | custom-call | flops 7549747200 | bytes 9175040 | tf_op jit(solution)/shard_map/to_grid/pallas_call | solution.py:246
  173.9 0.2 broadcast_in_dim.29
  174.1 12.9 %scatter_fusion = bf16[6400,128]{1,0:T(8,128)(2,1)S(1)} fusion(bf16[6400,128]{1,0:T(8,128)(2,1)S(1)} %broadcast_in_dim.29, s32[2880]{0:T(1024)S(1)} %compare_select_fusion.1, bf16[2880,128]{1,0:T(8,128)(2,1)} %get-tuple-element.39), kind=kCustom, calls=%fused_computation.2 | custom fusion | bytes 2223360 | tf_op jit(solution)/shard_map/scatter | solution.py:549
  187.1 0.0 all-to-all-done.1.coeff_ref
  187.1 0.0 copy-start.3
  187.1 0.1 compare_select_fusion.2
  187.2 0.7 copy-done.3
  187.9 4.3 to_grid.3
  192.2 2.6 scatter_fusion.1
  194.9 0.0 copy-start
  194.9 1.2 copy-done
  196.0 82.5 %network.1 = bf16[16,400,128]{2,1,0:T(8,128)(2,1)} custom-call(bf16[16,400,128]{2,1,0:T(8,128)(2,1)} %bitcast.12, bf16[1,128,1024]{2,1,0:T(8,128)(2,1)} %in_ref.1, bf16[1,1024,1024]{2,1,0:T(8,128)(2,1)} %mid_ref.1, bf16[1,1024,128]{2,1,0:T(8,128)(2,1)} %out_ref.1), custom_call_target="tpu_custom_call" | custom-call | flops 16777216000 | bytes 5373952 | tf_op jit(solution)/shard_map/network/pallas_call | solution.py:471
  278.5 3.3 gather_fusion.1
  281.8 0.0 copy-start.1
  281.8 4.4 to_fourier.3
  286.3 4.9 %all-to-all-start.3 = ((bf16[16,2,40,256]{3,2,1,0:T(8,128)(2,1)}), bf16[16,2,40,256]{3,2,1,0:T(8,128)(2,1)S(1)}, u32[]{:S(2)}, u32[]{:S(2)}) async-start(bf16[16,2,40,256]{3,2,1,0:T(8,128)(2,1)} %to_fourier.3), calls=%async_computation.3 | async-start | bytes 1310720 | tf_op jit(solution)/shard_map/all_to_all | solution.py:504
  291.2 0.0 copy-done.1
  291.2 7.1 %gather_fusion = bf16[2880,128]{1,0:T(8,128)(2,1)} fusion(bf16[6400,128]{1,0:T(8,128)(2,1)S(1)} %bitcast.16, s32[3072]{0:T(1024)S(1)} %pad_clamp_fusion), kind=kCustom, calls=%fused_computation | custom fusion | bytes 1486080 | tf_op jit(solution)/shard_map/gather | solution.py:556
  298.3 15.5 %to_fourier.2 = bf16[16,18,40,256]{3,2,1,0:T(8,128)(2,1)} custom-call(f32[18,1280,128]{2,1,0:T(8,128)} %get-tuple-element.34.forced_ref, bf16[2880,128]{1,0:T(8,128)(2,1)} %gather_fusion, bf16[1280,1280]{1,0:T(8,128)(2,1)} %get-tuple-element.45.table_ref), custom_call_target="tpu_custom_call" | custom-call | flops 7549747200 | bytes 15073280 | tf_op jit(solution)/shard_map/to_fourier/pallas_call | solution.py:299
  313.9 0.0 all-to-all-done.3.rest_1_
  313.9 0.0 copy-start.2
  313.9 136.6 %all_to_all.20.rest_0_ = bf16[16,18,40,256]{3,2,1,0:T(8,128)(2,1)} all-to-all(bf16[16,18,40,256]{3,2,1,0:T(8,128)(2,1)} %to_fourier.2), channel_id=1, replica_groups=mesh['grp'=2,'wave'=16] {'wave'}, dimensions={0} | all-to-all | bytes 11796480 | tf_op jit(solution)/shard_map/all_to_all | solution.py:504
  450.4 0.0 copy-done.2
  450.4 16.9 %forward_legendre.1 = bf16[20,641,256]{2,1,0:T(8,128)(2,1)} custom-call(s32[20]{0:T(128)} %dynamic_slice.3.low_ref, bf16[20,320,641]{2,1,0:T(8,128)(2,1)} %bitcast.14, bf16[256,256]{1,0:T(8,128)(2,1)} %fusion.10.order_ref, bf16[16,18,40,256]{3,2,1,0:T(8,128)(2,1)} %all_to_all.20.rest_0_, bf16[16,2,40,256]{3,2,1,0:T(8,128)(2,1)} %copy-done.2), custom_call_target="tpu_custom_call" | custom-call | flops 4200857600 | bytes 16409600 | tf_op jit(solution)/shard_map/forward_legendre/pallas_call | solution.py:365
  (17 shorter events, 0.2 us)
Async XLA Ops:
  17.4 7.5 %copy-start.5 = (s32[320]{0:T(512)S(1)}, s32[320]{0:T(512)}, u32[]{:S(2)}) copy-start(s32[320]{0:T(512)} %param.9) | copy-start | bytes 3844
  17.4 7.8 %copy-start.4 = (s32[3200,1]{0,1:T(1,128)S(1)}, s32[3200,1]{0,1:T(1,128)}, u32[]{:S(2)}) copy-start(s32[3200,1]{0,1:T(1,128)} %param.10) | copy-start | bytes 38404
  17.4 115.3 %all-to-all-start = ((bf16[16,18,40,256]{3,2,1,0:T(8,128)(2,1)}), bf16[16,18,40,256]{3,2,1,0:T(8,128)(2,1)}, u32[]{:S(2)}, u32[]{:S(2)}) async-start(bf16[16,18,40,256]{3,2,1,0:T(8,128)(2,1)} %get-tuple-element.28), calls=%async_computation | async-start | bytes 11796480 | tf_op jit(solution)/shard_map/all_to_all | solution.py:504
  132.7 54.4 %all-to-all-start.1 = ((bf16[16,2,40,256]{3,2,1,0:T(8,128)(2,1)}), bf16[16,2,40,256]{3,2,1,0:T(8,128)(2,1)S(1)}, u32[]{:S(2)}, u32[]{:S(2)}) async-start(bf16[16,2,40,256]{3,2,1,0:T(8,128)(2,1)} %get-tuple-element.35), calls=%async_computation.1 | async-start | bytes 1310720 | tf_op jit(solution)/shard_map/all_to_all | solution.py:504
  187.1 0.8 copy-start.3
  194.9 1.2 copy-start
  281.8 9.4 %copy-start.1 = (bf16[16,400,128]{2,1,0:T(8,128)(2,1)S(1)}, bf16[16,400,128]{2,1,0:T(8,128)(2,1)}, u32[]{:S(2)}) copy-start(bf16[16,400,128]{2,1,0:T(8,128)(2,1)} %network.1) | copy-start | bytes 4915204
  286.3 27.6 %all-to-all-start.3 = ((bf16[16,2,40,256]{3,2,1,0:T(8,128)(2,1)}), bf16[16,2,40,256]{3,2,1,0:T(8,128)(2,1)S(1)}, u32[]{:S(2)}, u32[]{:S(2)}) async-start(bf16[16,2,40,256]{3,2,1,0:T(8,128)(2,1)} %to_fourier.3), calls=%async_computation.3 | async-start | bytes 1310720 | tf_op jit(solution)/shard_map/all_to_all | solution.py:504
  313.9 136.6 %copy-start.2 = (bf16[16,2,40,256]{3,2,1,0:T(8,128)(2,1)}, bf16[16,2,40,256]{3,2,1,0:T(8,128)(2,1)S(1)}, u32[]{:S(2)}) copy-start(bf16[16,2,40,256]{3,2,1,0:T(8,128)(2,1)S(1)} %all-to-all-done.3.rest_1_) | copy-start | bytes 1966084
